TPU v7x, 32 devices: a whole 2x2x4 slice. The times are simulated.
32 devices in a mesh: grp: 2 (over x), gy: 16 (over z, y, core).
Axes of the slice: x: 2, y: 2, z: 4, core: 2. Of those that a mesh axis runs over, the one named last changes fastest.
Arguments:
- window_feats: bfloat16 [128, 32, 4, 16, 128], P(('grp', 'gy')), parts along dimension 0, may hold values from -6 to 6
- window_brick: int32 [128], P('grp'), parts along dimension 0, may hold values from 0 to 14, as said below
- window_z: int32 [128], P('grp'), parts along dimension 0, may hold values from 0 to 128, as said below
- window_count: int32 [32], P('grp'), parts along dimension 0, may hold values from 1 to 4, as said below
- gaussian: float32 [4, 16, 128], replicated, may hold values from 0.01 to 400, as said below
- brick_feats: bfloat16 [32, 4, 256, 256], P(None, None, ('grp', 'gy')), parts along dimension 2, may hold values from -85 to 85
- teacher_w1: bfloat16 [32, 32, 3, 3, 3], replicated, may hold values from -0.21875 to 0.21875
- teacher_w2: bfloat16 [16, 32, 3, 3, 3], replicated, may hold values from -0.21875 to 0.21875
- student_w1: bfloat16 [32, 32, 3, 3, 3], replicated, may hold values from -0.21875 to 0.21875
- student_w2: bfloat16 [16, 32, 3, 3, 3], replicated, may hold values from -0.21875 to 0.21875
Outputs:
- teacher_sum: float32 [16, 4, 256, 256], P(None, None, ('grp', 'gy')), parts along dimension 2
- feature_grad: float32 [32, 4, 256, 256], P(None, None, ('grp', 'gy')), parts along dimension 2
There are 2 independent parts, one for each index of `grp`. A program takes and returns all parts, laid end to end along the dimension named above; an argument that names none is the same for every part. Nothing has to cross between parts.
Inputs may be any that keep to these rules, and one draw needn't show every extreme that they name: `window_brick`: slot s names the brick owner s // 4 or the one before it, within 0 to 14. `window_z`: a multiple of 32. `window_count`: some owner has all 4 slots live. `gaussian`: positive.
All inputs are finite; a program needn't handle non-finite values.
Results may differ from a plain program's by a relative error of at most 0.0065.
Values may be sent and summed in bfloat16 or wider, within the bound.
No kernel may reach another device: no remote copies, remote signals or barrier semaphores. Data moves between devices by JAX's collectives and lax.ppermute only.
A program may use at most 128 MiB of HBM per device.

v0:
```python
import functools

import jax
import jax.numpy as jnp
from jax import lax
from jax.experimental import pallas as pl
from jax.experimental.pallas import tpu as pltpu
from jax.sharding import PartitionSpec as P

F32 = jnp.float32
BF16 = jnp.bfloat16
VMEM_BYTES = 56 * 1024 * 1024


def spread(channels, by_x):
    a = lax.broadcasted_iota(jnp.int32, (3, channels, 16 * channels), 0)
    c = lax.broadcasted_iota(jnp.int32, (3, channels, 16 * channels), 1)
    lane = lax.broadcasted_iota(jnp.int32, (3, channels, 16 * channels), 2)
    x = lane // (4 * channels)
    rest = lane % (4 * channels)
    if by_x:
        xi, ci = rest // channels, rest % channels
    else:
        xi, ci = rest % 4, rest // 4
    return ((ci == c) & (xi == x + a - 1)).astype(F32).astype(BF16)


def band(w_ref, hot_ref):
    _, taps, outs, ins = w_ref.shape
    wide = None
    for a in range(3):
        part = jnp.dot(
            w_ref[a].reshape(taps * outs, ins), hot_ref[a], preferred_element_type=F32
        )
        wide = part if wide is None else wide + part
    width = 4 * ins
    result = []
    for t in range(taps):
        rows = wide[t * outs : (t + 1) * outs]
        result.append(
            jnp.concatenate(
                [rows[:, x * width : (x + 1) * width] for x in range(4)], axis=0
            )
        )
    return result


def fill_big(big_ref, blocks, out_rows):
    rows, width = blocks[0].shape
    in_rows = out_rows + 2
    zero = jnp.zeros((rows, width), BF16)
    for yo in range(out_rows):
        for d in range(3):
            for yi in range(in_rows):
                b = yi - yo
                piece = blocks[b * 3 + d].astype(BF16) if 0 <= b < 3 else zero
                col = (d * in_rows + yi) * width
                big_ref[pl.ds(yo * rows, rows), pl.ds(col, width)] = piece


def shifted(v, step):
    lanes = v.shape[-1]
    rolled = pltpu.roll(v, (-step) % lanes, v.ndim - 1)
    lane = lax.broadcasted_iota(jnp.int32, v.shape, v.ndim - 1)
    edge = lane == (lanes - 1 if step > 0 else 0)
    return jnp.where(edge, 0.0, rolled)


def put_row(buf_ref, y, v):
    buf_ref[1, y] = v.astype(BF16)
    buf_ref[0, y] = shifted(v, -1).astype(BF16)
    buf_ref[2, y] = shifted(v, 1).astype(BF16)


def window(buf_ref, y, count):
    rows = buf_ref.shape[2]
    return jnp.concatenate(
        [buf_ref[d, pl.ds(y, count)].reshape(count * rows, -1) for d in range(3)], axis=0
    )


def sigmoid(v):
    return 0.5 + 0.5 * jnp.tanh(0.5 * v)


def teacher_kernel(
    brick_s,
    z_s,
    count_s,
    feats_ref,
    gauss_ref,
    w1_ref,
    w2_ref,
    hot1_ref,
    hot2_ref,
    own_ref,
    pair_ref,
    cross_ref,
    big1,
    big2,
    flat,
    xbuf,
    hbuf,
    total,
):
    slot = pl.program_id(0)
    slots = pl.num_programs(0)
    position = lax.axis_index("gy")
    lanes = 128

    @pl.when(slot == 0)
    def _():
        fill_big(big1, band(w1_ref, hot1_ref), 2)
        fill_big(big2, band(w2_ref, hot2_ref), 4)
        total[...] = jnp.zeros_like(total)
        for y in (0, 17):
            xbuf[:, y] = jnp.zeros((3, 128, lanes), BF16)
            hbuf[:, y] = jnp.zeros((3, 128, lanes), BF16)

    @pl.when(slot < count_s[position])
    def _():
        flat[...] = feats_ref[0].astype(F32)
        for y in range(16):
            put_row(xbuf, y + 1, flat[pl.ds(y, 128, stride=16), :])
        for y in range(0, 8, 2):
            both = jnp.concatenate([window(xbuf, y, 4), window(xbuf, y + 8, 4)], axis=1)
            pre = jnp.dot(big1[...], both, preferred_element_type=F32)
            hid = pre * sigmoid(pre)
            for half in range(2):
                for k in range(2):
                    put_row(
                        hbuf,
                        8 * half + y + k + 1,
                        hid[k * 128 : (k + 1) * 128, half * 128 : (half + 1) * 128],
                    )
        z0 = z_s[position * slots + slot]
        base = 8 * (brick_s[position * slots + slot] - position + 1)
        lane = lax.broadcasted_iota(jnp.int32, (64, lanes), 1)
        first = lane >= z0
        for y in range(0, 8, 4):
            both = jnp.concatenate([window(hbuf, y, 6), window(hbuf, y + 8, 6)], axis=1)
            logits = jnp.dot(big2[...], both, preferred_element_type=F32)
            for half in range(2):
                for k in range(4):
                    row = 8 * half + y + k
                    part = logits[k * 64 : (k + 1) * 64, half * 128 : (half + 1) * 128]
                    weight = jnp.concatenate(
                        [
                            jnp.broadcast_to(gauss_ref[x, row : row + 1, :], (16, lanes))
                            for x in range(4)
                        ],
                        axis=0,
                    )
                    turned = pltpu.roll(part * weight, lax.rem(z0, 128), 1)
                    total[base + row, :, pl.ds(0, 128)] += jnp.where(first, turned, 0.0)
                    total[base + row, :, pl.ds(128, 128)] += jnp.where(first, 0.0, turned)

    @pl.when(slot == slots - 1)
    def _():
        odd = lax.rem(position, 2)
        own_ref[...] = total[8:16]
        pair_ref[...] = total[pl.ds(16 * (1 - odd), 8)]
        cross_ref[...] = total[pl.ds(16 * odd, 8)]


def teacher(brick, z, count, feats, gauss, w1, w2, hot1, hot2):
    slots = feats.shape[0]
    whole = lambda a: pl.BlockSpec(a.shape, lambda s, *_: (0,) * a.ndim)
    sums = jax.ShapeDtypeStruct((8, 64, 256), F32)
    out_spec = pl.BlockSpec((8, 64, 256), lambda s, *_: (0, 0, 0))
    return pl.pallas_call(
        teacher_kernel,
        name="teacher",
        grid_spec=pltpu.PrefetchScalarGridSpec(
            num_scalar_prefetch=3,
            grid=(slots,),
            in_specs=[
                pl.BlockSpec((1, 2048, 128), lambda s, *_: (s, 0, 0)),
                whole(gauss),
                whole(w1),
                whole(w2),
                whole(hot1),
                whole(hot2),
            ],
            out_specs=[out_spec] * 3,
            scratch_shapes=[
                pltpu.VMEM((256, 1536), BF16),
                pltpu.VMEM((256, 2304), BF16),
                pltpu.VMEM((2048, 128), F32),
                pltpu.VMEM((3, 18, 128, 128), BF16),
                pltpu.VMEM((3, 18, 128, 128), BF16),
                pltpu.VMEM((24, 64, 256), F32),
            ],
        ),
        out_shape=[sums] * 3,
        compiler_params=pltpu.CompilerParams(
            dimension_semantics=("arbitrary",), vmem_limit_bytes=VMEM_BYTES
        ),
        cost_estimate=pl.CostEstimate(
            flops=11_000_000_000, bytes_accessed=4_000_000, transcendentals=1_000_000
        ),
    )(brick, z, count, feats, gauss, w1, w2, hot1, hot2)


def relay_kernel(feats_ref, main_ref, pair_ref, cross_ref, flat):
    odd = lax.rem(lax.axis_index("gy"), 2)
    for h in range(2):
        flat[...] = feats_ref[:, pl.ds(h * 128, 128)].astype(F32)
        for y in range(8):
            main_ref[y, :, pl.ds(h * 128, 128)] = flat[pl.ds(y, 128, stride=8), :].astype(BF16)
    pair_ref[...] = main_ref[pl.ds(6 * (1 - odd), 2)]
    cross_ref[...] = main_ref[pl.ds(6 * odd, 2)]


def relay(feats):
    edge = jax.ShapeDtypeStruct((2, 128, 256), BF16)
    return pl.pallas_call(
        relay_kernel,
        name="relay",
        out_shape=[jax.ShapeDtypeStruct((8, 128, 256), BF16), edge, edge],
        scratch_shapes=[pltpu.VMEM((1024, 128), F32)],
        compiler_params=pltpu.CompilerParams(vmem_limit_bytes=VMEM_BYTES),
        cost_estimate=pl.CostEstimate(flops=0, bytes_accessed=1_500_000, transcendentals=0),
    )(feats)


def put_edges(store, pair_ref, cross_ref, low, high):
    odd = lax.rem(lax.axis_index("gy"), 2)
    pair_at = jnp.where(odd == 1, low, high)
    cross_at = jnp.where(odd == 1, high, low)
    for k in range(2):
        store(pair_at + k, pair_ref[k])
        store(cross_at + k, cross_ref[k])


def inside(y):
    position = lax.axis_index("gy")
    last = lax.axis_size("gy") - 1
    if y < 0:
        return jnp.where(position > 0, 1.0, 0.0)
    if y >= 8:
        return jnp.where(position < last, 1.0, 0.0)
    return None


def class_softmax(v):
    parts = []
    for x in range(4):
        block = v[x * 16 : (x + 1) * 16]
        peak = jnp.max(block, axis=0, keepdims=True)
        grown = jnp.exp(block - peak)
        parts.append(grown / jnp.sum(grown, axis=0, keepdims=True))
    return jnp.concatenate(parts, axis=0)


def forward_kernel(
    main_ref,
    pair_ref,
    cross_ref,
    w1_ref,
    w2_ref,
    hot1_ref,
    hot2_ref,
    prob_ref,
    slope_ref,
    big1,
    big2,
    xbuf,
    hbuf,
):
    fill_big(big1, band(w1_ref, hot1_ref), 2)
    fill_big(big2, band(w2_ref, hot2_ref), 4)
    store = lambda y, v: put_row(xbuf, y, v.astype(F32))
    for y in range(8):
        store(y + 2, main_ref[y])
    put_edges(store, pair_ref, cross_ref, 0, 10)
    for y in range(0, 10, 2):
        pre = jnp.dot(big1[...], window(xbuf, y, 4), preferred_element_type=F32)
        sig = sigmoid(pre)
        hid = pre * sig
        slope = sig * (1.0 + pre * (1.0 - sig))
        for k in range(2):
            row = y + k
            rows = slice(k * 128, (k + 1) * 128)
            slope_ref[row] = slope[rows]
            keep = inside(row - 1)
            put_row(hbuf, row, hid[rows] if keep is None else hid[rows] * keep)
    for y in range(0, 8, 4):
        logits = jnp.dot(big2[...], window(hbuf, y, 6), preferred_element_type=F32)
        for k in range(4):
            prob_ref[y + k] = class_softmax(logits[k * 64 : (k + 1) * 64])


def forward(main, pair, cross, w1, w2, hot1, hot2):
    return pl.pallas_call(
        forward_kernel,
        name="forward",
        out_shape=[
            jax.ShapeDtypeStruct((8, 64, 256), F32),
            jax.ShapeDtypeStruct((10, 128, 256), F32),
        ],
        scratch_shapes=[
            pltpu.VMEM((256, 1536), BF16),
            pltpu.VMEM((256, 2304), BF16),
            pltpu.VMEM((3, 12, 128, 256), BF16),
            pltpu.VMEM((3, 10, 128, 256), BF16),
        ],
        compiler_params=pltpu.CompilerParams(vmem_limit_bytes=VMEM_BYTES),
        cost_estimate=pl.CostEstimate(
            flops=4_000_000_000, bytes_accessed=3_000_000, transcendentals=500_000
        ),
    )(main, pair, cross, w1, w2, hot1, hot2)


def combine_kernel(
    own_ref,
    from_pair_ref,
    from_cross_ref,
    prob_ref,
    sum_ref,
    main_ref,
    pair_ref,
    cross_ref,
    turn0,
    turn1,
):
    odd = lax.rem(lax.axis_index("gy"), 2)
    for y in range(8):
        value = own_ref[y] + from_pair_ref[y] + from_cross_ref[y]
        for x in range(4):
            for h, turn in enumerate((turn0, turn1)):
                turn[pl.ds(x * 8 + y, 16, stride=32), :] = value[
                    x * 16 : (x + 1) * 16, h * 128 : (h + 1) * 128
                ]
        main_ref[y] = (prob_ref[y] - class_softmax(value)).astype(BF16)
    pair_ref[...] = main_ref[pl.ds(6 * (1 - odd), 2)]
    cross_ref[...] = main_ref[pl.ds(6 * odd, 2)]
    sum_ref[:, pl.ds(0, 128)] = turn0[...]
    sum_ref[:, pl.ds(128, 128)] = turn1[...]


def combine(own, from_pair, from_cross, prob):
    edge = jax.ShapeDtypeStruct((2, 64, 256), BF16)
    return pl.pallas_call(
        combine_kernel,
        name="combine",
        out_shape=[
            jax.ShapeDtypeStruct((512, 256), F32),
            jax.ShapeDtypeStruct((8, 64, 256), BF16),
            edge,
            edge,
        ],
        scratch_shapes=[pltpu.VMEM((512, 128), F32)] * 2,
        compiler_params=pltpu.CompilerParams(vmem_limit_bytes=VMEM_BYTES),
        cost_estimate=pl.CostEstimate(
            flops=1_000_000, bytes_accessed=3_000_000, transcendentals=200_000
        ),
    )(own, from_pair, from_cross, prob)


def backward_kernel(
    main_ref,
    pair_ref,
    cross_ref,
    slope_ref,
    w1_ref,
    w2_ref,
    hot1_ref,
    hot2_ref,
    out_ref,
    big1,
    big2,
    gbuf,
    pbuf,
    turn0,
    turn1,
):
    flip1 = band(w1_ref, hot1_ref)
    fill_big(big1, [flip1[8 - t].T for t in range(9)], 2)
    flip2 = band(w2_ref, hot2_ref)
    fill_big(big2, [flip2[8 - t].T for t in range(9)], 2)
    store = lambda y, v: put_row(gbuf, y, v.astype(F32))
    for y in range(8):
        store(y + 2, main_ref[y])
    put_edges(store, pair_ref, cross_ref, 0, 10)
    for y in range(0, 10, 2):
        grad = jnp.dot(big2[...], window(gbuf, y, 4), preferred_element_type=F32)
        for k in range(2):
            row = y + k
            pre_grad = grad[k * 128 : (k + 1) * 128] * slope_ref[row]
            keep = inside(row - 1)
            put_row(pbuf, row, pre_grad if keep is None else pre_grad * keep)
    for y in range(0, 8, 2):
        grad = jnp.dot(big1[...], window(pbuf, y, 4), preferred_element_type=F32)
        for k in range(2):
            for x in range(4):
                for h, turn in enumerate((turn0, turn1)):
                    at = k * 128 + x * 32
                    turn[pl.ds(x * 8 + y + k, 32, stride=32), :] = grad[
                        at : at + 32, h * 128 : (h + 1) * 128
                    ]
    out_ref[:, pl.ds(0, 128)] = turn0[...]
    out_ref[:, pl.ds(128, 128)] = turn1[...]


def backward(main, pair, cross, slope, w1, w2, hot1, hot2):
    return pl.pallas_call(
        backward_kernel,
        name="backward",
        out_shape=jax.ShapeDtypeStruct((1024, 256), F32),
        scratch_shapes=[
            pltpu.VMEM((256, 1536), BF16),
            pltpu.VMEM((256, 768), BF16),
            pltpu.VMEM((3, 12, 64, 256), BF16),
            pltpu.VMEM((3, 10, 128, 256), BF16),
            pltpu.VMEM((1024, 128), F32),
            pltpu.VMEM((1024, 128), F32),
        ],
        compiler_params=pltpu.CompilerParams(vmem_limit_bytes=VMEM_BYTES),
        cost_estimate=pl.CostEstimate(
            flops=4_000_000_000, bytes_accessed=3_000_000, transcendentals=0
        ),
    )(main, pair, cross, slope, w1, w2, hot1, hot2)


def swap_pair(value):
    count = lax.axis_size("gy")
    return lax.ppermute(value, "gy", [(i, i ^ 1) for i in range(count)])


def swap_cross(value):
    count = lax.axis_size("gy")
    pairs = [(i, i + 1) for i in range(1, count - 1, 2)]
    return lax.ppermute(value, "gy", pairs + [(j, i) for i, j in pairs])


def taps_first(w):
    outs, ins = w.shape[:2]
    return jnp.transpose(w, (2, 3, 4, 0, 1)).reshape(3, 9, outs, ins)


def body(
    window_feats,
    window_brick,
    window_z,
    window_count,
    gaussian,
    brick_feats,
    teacher_w1,
    teacher_w2,
    student_w1,
    student_w2,
):
    tw1, tw2, sw1, sw2 = map(taps_first, (teacher_w1, teacher_w2, student_w1, student_w2))
    hot_c = spread(32, False)
    hot_x = spread(32, True)
    main, to_pair, to_cross = relay(brick_feats.reshape(1024, 256))
    edge_cross = swap_cross(to_cross)
    edge_pair = swap_pair(to_pair)
    own, sum_pair, sum_cross = teacher(
        window_brick,
        window_z,
        window_count,
        window_feats.reshape(window_feats.shape[0], 2048, 128),
        gaussian,
        tw1,
        tw2,
        hot_c,
        hot_x,
    )
    got_cross = swap_cross(sum_cross)
    got_pair = swap_pair(sum_pair)
    prob, slope = forward(main, edge_pair, edge_cross, sw1, sw2, hot_c, hot_x)
    teacher_sum, grad, grad_pair, grad_cross = combine(own, got_pair, got_cross, prob)
    near_cross = swap_cross(grad_cross)
    near_pair = swap_pair(grad_pair)
    feature_grad = backward(grad, near_pair, near_cross, slope, sw1, sw2, hot_x, hot_x)
    return (teacher_sum.reshape(16, 4, 8, 256), feature_grad.reshape(32, 4, 8, 256))


def solution(mesh):
    placed = (
        P(("grp", "gy"), None, None, None, None),
        P("grp"),
        P("grp"),
        P("grp"),
        P(),
        P(None, None, ("grp", "gy"), None),
        P(),
        P(),
        P(),
        P(),
    )
    return jax.shard_map(
        body,
        mesh=mesh,
        in_specs=placed,
        out_specs=(P(None, None, ("grp", "gy"), None), P(None, None, ("grp", "gy"), None)),
        check_vma=False,
    )
```

profile of v0, /device:TPU:7, one launch (start us, length us, event | category | flops | bytes accessed | tf_op | source)
XLA Modules:
  0.0 57.0 jit_solution(4473106219325393521)
XLA Ops:
  0.7 0.7 %convert_convert_fusion = (bf16[3,32,512]{2,1,0:T(8,128)(2,1)}, bf16[3,32,512]{2,1,0:T(8,128)(2,1)}) fusion(s32[512]{0:T(512)S(1)} %get-tuple-element.28, s32[512]{0:T(512)S(1)} %get-tuple-element.31, s32[512]{0:T(512)S(1)} %get-tuple-element.29, s32[512]{0:T(512)S(1)} %get-tuple-element.30, pred[512]{0:T(512)(128)(4,1)S(1)} %get-tuple-element.32, ...), kind=kLoop, calls=%fused_computation.21 | loop fusion | flops 2310144 | bytes 205824 | tf_op jit(solution)/shard_map/convert_element_type | solution.py:25
  1.4 13.2 %teacher.1 = (f32[8,64,256]{2,1,0:T(8,128)}, f32[8,64,256]{2,1,0:T(8,128)}, f32[8,64,256]{2,1,0:T(8,128)}) custom-call(s32[64]{0:T(128)} %brick_s.1, s32[64]{0:T(128)} %z_s.1, s32[16]{0:T(128)} %count_s.1, bf16[4,2048,128]{2,1,0:T(8,128)(2,1)} %bitcast.17, f32[4,16,128]{2,1,0:T(8,128)} %gauss_ref.1, bf16[3,9,32,32]{3,2,1,0:T(8,128)(2,1)} %bitcast.19, ...), custom_call_target="tpu_custom_call" | custom-call | flops 11000000512 | bytes 4000000 | tf_op jit(solution)/shard_map/teacher/pallas_call | solution.py:171
  14.6 0.7 %collective-permute-start = (f32[8,64,256]{2,1,0:T(8,128)}, f32[8,64,256]{2,1,0:T(8,128)S(1)}, u32[]{:S(2)}, u32[]{:S(2)}) collective-permute-start(f32[8,64,256]{2,1,0:T(8,128)} %get-tuple-element.15), channel_id=1, source_target_pairs={{0,1},{1,0},{2,3},{3,2},{4,5},{5,4},{6,7},{7,6},{8,9},{9,8},{10,11... | collective-permute-start | bytes 1572872 | tf_op jit(solution)/shard_map/ppermute | solution.py:428
  15.3 3.0 %collective-permute-start.1 = (f32[8,64,256]{2,1,0:T(8,128)}, f32[8,64,256]{2,1,0:T(8,128)S(1)}, u32[]{:S(2)}, u32[]{:S(2)}) collective-permute-start(f32[8,64,256]{2,1,0:T(8,128)} %get-tuple-element.16), channel_id=1, source_target_pairs={{1,2},{3,4},{5,6},{7,8},{9,10},{11,12},{13,14},{2,1},{4,3},{6,5},{... | collective-permute-start | bytes 1572872 | tf_op jit(solution)/shard_map/ppermute | solution.py:434
  18.3 2.2 %relay.1 = (bf16[8,128,256]{2,1,0:T(8,128)(2,1)}, bf16[2,128,256]{2,1,0:T(8,128)(2,1)}, bf16[2,128,256]{2,1,0:T(8,128)(2,1)}) custom-call(bf16[1024,256]{1,0:T(8,128)(2,1)} %bitcast.16), custom_call_target="tpu_custom_call" | custom-call | bytes 1500000 | tf_op jit(solution)/shard_map/relay/pallas_call | solution.py:217
  20.5 0.0 collective-permute-start.2
  20.5 3.4 %collective-permute-start.3 = (bf16[2,128,256]{2,1,0:T(8,128)(2,1)}, bf16[2,128,256]{2,1,0:T(8,128)(2,1)S(1)}, u32[]{:S(2)}, u32[]{:S(2)}) collective-permute-start(bf16[2,128,256]{2,1,0:T(8,128)(2,1)} %get-tuple-element.19), channel_id=1, source_target_pairs={{1,2},{3,4},{5,6},{7,8},{9,10},{11,12},{13,14},{2,1},{4,3},{6,5},{... | collective-permute-start | bytes 393224 | tf_op jit(solution)/shard_map/ppermute | solution.py:434
  23.9 0.0 collective-permute-done.2.pair_ref
  23.9 0.0 copy-start.2
  23.9 4.5 %collective-permute-done.3.cross_ref = bf16[2,128,256]{2,1,0:T(8,128)(2,1)S(1)} collective-permute-done((bf16[2,128,256]{2,1,0:T(8,128)(2,1)}, bf16[2,128,256]{2,1,0:T(8,128)(2,1)S(1)}, u32[]{:S(2)}, u32[]{:S(2)}) %collective-permute-start.3) | collective-permute-done | bytes 131104 | tf_op jit(solution)/shard_map/ppermute | solution.py:434
  28.4 0.0 copy-start.3
  28.4 0.0 copy-done.2
  28.4 0.6 %copy-done.3 = bf16[2,128,256]{2,1,0:T(8,128)(2,1)} copy-done((bf16[2,128,256]{2,1,0:T(8,128)(2,1)}, bf16[2,128,256]{2,1,0:T(8,128)(2,1)S(1)}, u32[]{:S(2)}) %copy-start.3) | copy-done | bytes 131096
  29.0 4.8 %forward.1 = (f32[8,64,256]{2,1,0:T(8,128)}, f32[10,128,256]{2,1,0:T(8,128)}) custom-call(bf16[8,128,256]{2,1,0:T(8,128)(2,1)} %get-tuple-element.17.main_ref, bf16[2,128,256]{2,1,0:T(8,128)(2,1)} %copy-done.2, bf16[2,128,256]{2,1,0:T(8,128)(2,1)} %copy-done.3, bf16[3,9,32,32]{3,2,1,0:T(8,128)(2,1)} %bitcast.20, bf16[3,9,16,32]{3,2,1,0:T(8,128)(2,1)} %bitcast.23, ...), custom_call_target="tpu_custom_call" | custom-call | flops 4000000000 | bytes 3000000 | tf_op jit(solution)/shard_map/forward/pallas_call | solution.py:295
  33.9 0.0 collective-permute-done.from_pair_ref
  33.9 0.0 copy-start
  33.9 0.0 collective-permute-done.1.from_cross_ref
  33.9 0.0 copy-start.1
  33.9 0.8 %copy-done = f32[8,64,256]{2,1,0:T(8,128)} copy-done((f32[8,64,256]{2,1,0:T(8,128)}, f32[8,64,256]{2,1,0:T(8,128)S(1)}, u32[]{:S(2)}) %copy-start) | copy-done | bytes 524312
  34.7 0.2 copy-done.1
  34.8 3.1 %combine.1 = (f32[512,256]{1,0:T(8,128)}, bf16[8,64,256]{2,1,0:T(8,128)(2,1)}, bf16[2,64,256]{2,1,0:T(8,128)(2,1)}, bf16[2,64,256]{2,1,0:T(8,128)(2,1)}) custom-call(f32[8,64,256]{2,1,0:T(8,128)} %get-tuple-element.14.own_ref, f32[8,64,256]{2,1,0:T(8,128)} %copy-done, f32[8,64,256]{2,1,0:T(8,128)} %copy-done.1, f32[8,64,256]{2,1,0:T(8,128)} %get-tuple-element.20.prob_ref), custom_call_target="tpu_custom_call" | custom-call | flops 1000000 | bytes 3000000 | tf_op jit(solution)/shard_map/combine/pallas_call | solution.py:344
  38.0 6.0 %collective-permute-start.4 = (bf16[2,64,256]{2,1,0:T(8,128)(2,1)}, bf16[2,64,256]{2,1,0:T(8,128)(2,1)S(1)}, u32[]{:S(2)}, u32[]{:S(2)}) collective-permute-start(bf16[2,64,256]{2,1,0:T(8,128)(2,1)} %get-tuple-element.23), channel_id=1, source_target_pairs={{0,1},{1,0},{2,3},{3,2},{4,5},{5,4},{6,7},{7,6},{8,9},{9,8},{10,11... | collective-permute-start | bytes 196616 | tf_op jit(solution)/shard_map/ppermute | solution.py:428
  44.0 3.5 %collective-permute-start.5 = (bf16[2,64,256]{2,1,0:T(8,128)(2,1)}, bf16[2,64,256]{2,1,0:T(8,128)(2,1)S(1)}, u32[]{:S(2)}, u32[]{:S(2)}) collective-permute-start(bf16[2,64,256]{2,1,0:T(8,128)(2,1)} %get-tuple-element.24), channel_id=1, source_target_pairs={{1,2},{3,4},{5,6},{7,8},{9,10},{11,12},{13,14},{2,1},{4,3},{6,5},{... | collective-permute-start | bytes 196616 | tf_op jit(solution)/shard_map/ppermute | solution.py:434
  47.5 0.0 collective-permute-done.4.pair_ref
  47.5 0.0 copy-start.4
  47.6 3.1 %collective-permute-done.5.cross_ref = bf16[2,64,256]{2,1,0:T(8,128)(2,1)S(1)} collective-permute-done((bf16[2,64,256]{2,1,0:T(8,128)(2,1)}, bf16[2,64,256]{2,1,0:T(8,128)(2,1)S(1)}, u32[]{:S(2)}, u32[]{:S(2)}) %collective-permute-start.5) | collective-permute-done | bytes 65568 | tf_op jit(solution)/shard_map/ppermute | solution.py:434
  50.7 0.0 copy-start.5
  50.7 0.0 copy-done.4
  50.7 0.6 %copy-done.5 = bf16[2,64,256]{2,1,0:T(8,128)(2,1)} copy-done((bf16[2,64,256]{2,1,0:T(8,128)(2,1)}, bf16[2,64,256]{2,1,0:T(8,128)(2,1)S(1)}, u32[]{:S(2)}) %copy-start.5) | copy-done | bytes 65560
  51.3 5.7 %backward.1 = f32[1024,256]{1,0:T(8,128)} custom-call(bf16[8,64,256]{2,1,0:T(8,128)(2,1)} %get-tuple-element.22.main_ref, bf16[2,64,256]{2,1,0:T(8,128)(2,1)} %copy-done.4, bf16[2,64,256]{2,1,0:T(8,128)(2,1)} %copy-done.5, f32[10,128,256]{2,1,0:T(8,128)} %get-tuple-element.25.slope_ref, bf16[3,9,32,32]{3,2,1,0:T(8,128)(2,1)} %bitcast.21, ...), custom_call_target="tpu_custom_call" | custom-call | flops 4000000000 | bytes 3000000 | tf_op jit(solution)/shard_map/backward/pallas_call | solution.py:407
  (3 shorter events, 0.0 us)
Async XLA Ops:
  14.6 19.3 %collective-permute-start = (f32[8,64,256]{2,1,0:T(8,128)}, f32[8,64,256]{2,1,0:T(8,128)S(1)}, u32[]{:S(2)}, u32[]{:S(2)}) collective-permute-start(f32[8,64,256]{2,1,0:T(8,128)} %get-tuple-element.15), channel_id=1, source_target_pairs={{0,1},{1,0},{2,3},{3,2},{4,5},{5,4},{6,7},{7,6},{8,9},{9,8},{10,11... | collective-permute-start | bytes 1572872 | tf_op jit(solution)/shard_map/ppermute | solution.py:428
  15.3 18.6 %collective-permute-start.1 = (f32[8,64,256]{2,1,0:T(8,128)}, f32[8,64,256]{2,1,0:T(8,128)S(1)}, u32[]{:S(2)}, u32[]{:S(2)}) collective-permute-start(f32[8,64,256]{2,1,0:T(8,128)} %get-tuple-element.16), channel_id=1, source_target_pairs={{1,2},{3,4},{5,6},{7,8},{9,10},{11,12},{13,14},{2,1},{4,3},{6,5},{... | collective-permute-start | bytes 1572872 | tf_op jit(solution)/shard_map/ppermute | solution.py:434
  20.5 3.4 %collective-permute-start.2 = (bf16[2,128,256]{2,1,0:T(8,128)(2,1)}, bf16[2,128,256]{2,1,0:T(8,128)(2,1)S(1)}, u32[]{:S(2)}, u32[]{:S(2)}) collective-permute-start(bf16[2,128,256]{2,1,0:T(8,128)(2,1)} %get-tuple-element.18), channel_id=1, source_target_pairs={{0,1},{1,0},{2,3},{3,2},{4,5},{5,4},{6,7},{7,6},{8,9},{9,8},{10,11... | collective-permute-start | bytes 393224 | tf_op jit(solution)/shard_map/ppermute | solution.py:428
  20.5 7.9 %collective-permute-start.3 = (bf16[2,128,256]{2,1,0:T(8,128)(2,1)}, bf16[2,128,256]{2,1,0:T(8,128)(2,1)S(1)}, u32[]{:S(2)}, u32[]{:S(2)}) collective-permute-start(bf16[2,128,256]{2,1,0:T(8,128)(2,1)} %get-tuple-element.19), channel_id=1, source_target_pairs={{1,2},{3,4},{5,6},{7,8},{9,10},{11,12},{13,14},{2,1},{4,3},{6,5},{... | collective-permute-start | bytes 393224 | tf_op jit(solution)/shard_map/ppermute | solution.py:434
  23.9 4.5 %copy-start.2 = (bf16[2,128,256]{2,1,0:T(8,128)(2,1)}, bf16[2,128,256]{2,1,0:T(8,128)(2,1)S(1)}, u32[]{:S(2)}) copy-start(bf16[2,128,256]{2,1,0:T(8,128)(2,1)S(1)} %collective-permute-done.2.pair_ref) | copy-start | bytes 393220
  28.4 0.6 %copy-start.3 = (bf16[2,128,256]{2,1,0:T(8,128)(2,1)}, bf16[2,128,256]{2,1,0:T(8,128)(2,1)S(1)}, u32[]{:S(2)}) copy-start(bf16[2,128,256]{2,1,0:T(8,128)(2,1)S(1)} %collective-permute-done.3.cross_ref) | copy-start | bytes 393220
  33.9 0.8 %copy-start = (f32[8,64,256]{2,1,0:T(8,128)}, f32[8,64,256]{2,1,0:T(8,128)S(1)}, u32[]{:S(2)}) copy-start(f32[8,64,256]{2,1,0:T(8,128)S(1)} %collective-permute-done.from_pair_ref) | copy-start | bytes 1572868
  33.9 1.0 %copy-start.1 = (f32[8,64,256]{2,1,0:T(8,128)}, f32[8,64,256]{2,1,0:T(8,128)S(1)}, u32[]{:S(2)}) copy-start(f32[8,64,256]{2,1,0:T(8,128)S(1)} %collective-permute-done.1.from_cross_ref) | copy-start | bytes 1572868
  38.0 9.6 %collective-permute-start.4 = (bf16[2,64,256]{2,1,0:T(8,128)(2,1)}, bf16[2,64,256]{2,1,0:T(8,128)(2,1)S(1)}, u32[]{:S(2)}, u32[]{:S(2)}) collective-permute-start(bf16[2,64,256]{2,1,0:T(8,128)(2,1)} %get-tuple-element.23), channel_id=1, source_target_pairs={{0,1},{1,0},{2,3},{3,2},{4,5},{5,4},{6,7},{7,6},{8,9},{9,8},{10,11... | collective-permute-start | bytes 196616 | tf_op jit(solution)/shard_map/ppermute | solution.py:428
  44.0 6.7 %collective-permute-start.5 = (bf16[2,64,256]{2,1,0:T(8,128)(2,1)}, bf16[2,64,256]{2,1,0:T(8,128)(2,1)S(1)}, u32[]{:S(2)}, u32[]{:S(2)}) collective-permute-start(bf16[2,64,256]{2,1,0:T(8,128)(2,1)} %get-tuple-element.24), channel_id=1, source_target_pairs={{1,2},{3,4},{5,6},{7,8},{9,10},{11,12},{13,14},{2,1},{4,3},{6,5},{... | collective-permute-start | bytes 196616 | tf_op jit(solution)/shard_map/ppermute | solution.py:434
  47.5 3.1 %copy-start.4 = (bf16[2,64,256]{2,1,0:T(8,128)(2,1)}, bf16[2,64,256]{2,1,0:T(8,128)(2,1)S(1)}, u32[]{:S(2)}) copy-start(bf16[2,64,256]{2,1,0:T(8,128)(2,1)S(1)} %collective-permute-done.4.pair_ref) | copy-start | bytes 196612
  50.7 0.6 %copy-start.5 = (bf16[2,64,256]{2,1,0:T(8,128)(2,1)}, bf16[2,64,256]{2,1,0:T(8,128)(2,1)S(1)}, u32[]{:S(2)}) copy-start(bf16[2,64,256]{2,1,0:T(8,128)(2,1)S(1)} %collective-permute-done.5.cross_ref) | copy-start | bytes 196612
where the time goes:
time: 57.4 us; the launch traced here: 57 us
  Pallas kernels  29 us (51%)
  starting transfers between devices  16.7 us (29%)
  waiting for transfers between devices  7.6 us (13%)
  local copies, waits for them, and re-layouts  2.23 us (4%)
  other arithmetic  0.75 us (1%)
  between operations  0.73 us (1%)
    pallas_call x1, Pallas kernels, teacher(): pl.pallas_call(teacher_kernel, name='teacher', grid_spec=pltpu.PrefetchSc...  13.2 us
    ppermute x3, starting transfers between devices, swap_cross(): return lax.ppermute(value, 'gy', pairs + [(j, i) for i, j in pairs])  9.96 us
    ppermute x3, waiting for transfers between devices, swap_cross(): return lax.ppermute(value, 'gy', pairs + [(j, i) for i, j in pairs])  7.59 us
    ppermute x3, starting transfers between devices, swap_pair(): return lax.ppermute(value, 'gy', [(i, i ^ 1) for i in range(count)])  6.7 us
    pallas_call x1, Pallas kernels, backward(): pl.pallas_call(backward_kernel, name='backward', out_shape=jax.ShapeDtype...  5.71 us
    pallas_call x1, Pallas kernels, forward(): pl.pallas_call(forward_kernel, name='forward', out_shape=[jax.ShapeDtypeS...  4.83 us
    pallas_call x1, Pallas kernels, combine(): pl.pallas_call(combine_kernel, name='combine', out_shape=[jax.ShapeDtypeS...  3.13 us
    unnamed x12, local copies, waits for them, and re-layouts  2.23 us
  transfers between devices with their start and end apart: 6, of which 2 were waited for; matrix products, arithmetic and copies ran while one was open for 0% of the time, Pallas kernels for 12%

commit v1 on v0

v1 whole, which is shorter than its diff:
```python
import functools

import jax
import jax.numpy as jnp
from jax import lax
from jax.experimental import pallas as pl
from jax.experimental.pallas import tpu as pltpu
from jax.sharding import PartitionSpec as P

F32 = jnp.float32
PITCH = 24
BF16 = jnp.bfloat16
VMEM = pl.BlockSpec(memory_space=pltpu.VMEM)
HBM = pl.BlockSpec(memory_space=pltpu.HBM)


def in_hbm(value):
    return pltpu.with_memory_space_constraint(value, pltpu.HBM)


def params(mib):
    return pltpu.CompilerParams(vmem_limit_bytes=mib * 1024 * 1024)


def cost(flops, moved):
    return pl.CostEstimate(flops=flops, bytes_accessed=moved, transcendentals=0)


def spread(ins, a, by_x):
    c = lax.broadcasted_iota(jnp.int32, (ins, 16 * ins), 0)
    lane = lax.broadcasted_iota(jnp.int32, (ins, 16 * ins), 1)
    x = lane // (4 * ins)
    rest = lane % (4 * ins)
    if by_x:
        xi, ci = rest // ins, rest % ins
    else:
        xi, ci = rest % 4, rest // 4
    return jnp.where((ci == c) & (xi == x + a - 1), 1.0, 0.0).astype(BF16)


def band(w_ref, by_x):
    _, taps, outs, ins = w_ref.shape
    wide = None
    for a in range(3):
        part = jnp.dot(
            w_ref[a].reshape(taps * outs, ins),
            spread(ins, a, by_x),
            preferred_element_type=F32,
        )
        wide = part if wide is None else wide + part
    width = 4 * ins
    result = []
    for t in range(taps):
        rows = wide[t * outs : (t + 1) * outs]
        result.append(
            jnp.concatenate(
                [rows[:, x * width : (x + 1) * width] for x in range(4)], axis=0
            )
        )
    return result


def fill_big(big_ref, blocks, out_rows):
    rows, width = blocks[0].shape
    in_rows = out_rows + 2
    zero = jnp.zeros((rows, width), BF16)
    for yo in range(out_rows):
        for d in range(3):
            for yi in range(in_rows):
                b = yi - yo
                piece = blocks[b * 3 + d].astype(BF16) if 0 <= b < 3 else zero
                col = (d * in_rows + yi) * width
                big_ref[pl.ds(yo * rows, rows), pl.ds(col, width)] = piece


def shifted(v, step):
    lanes = v.shape[-1]
    rolled = pltpu.roll(v, (-step) % lanes, v.ndim - 1)
    lane = lax.broadcasted_iota(jnp.int32, v.shape, v.ndim - 1)
    edge = lane == (lanes - 1 if step > 0 else 0)
    return jnp.where(edge, 0.0, rolled)


def put_row(buf_ref, y, v, lane=0):
    lanes = pl.ds(lane, v.shape[-1])
    buf_ref[1, y, :, lanes] = v.astype(BF16)
    buf_ref[0, y, :, lanes] = shifted(v, -1).astype(BF16)
    buf_ref[2, y, :, lanes] = shifted(v, 1).astype(BF16)


def window(buf_ref, y, count):
    rows = buf_ref.shape[2]
    return jnp.concatenate(
        [buf_ref[d, pl.ds(y, count)].reshape(count * rows, -1) for d in range(3)], axis=0
    )


def sigmoid(v):
    return 0.5 + 0.5 * jnp.tanh(0.5 * v)


def parity():
    return lax.rem(lax.axis_index("gy"), 2)


def teacher_half(
    own, tables, ready, feats_ref, gauss_ref, big1, big2, store, flat, xbuf, hbuf
):
    brick_s, z_s, count_s = tables
    position = lax.axis_index("gy")
    slots = feats_ref.shape[0]
    lanes = 128
    count = count_s[position]
    lane = lax.broadcasted_iota(jnp.int32, (64, lanes), 1)
    z0, mine, base = [], [], []
    for s in range(slots):
        slot = position * slots + s
        z0.append(z_s[slot])
        mine.append(brick_s[slot] == position)
        base.append(jnp.where(mine[s], 0, 8) if own else jnp.where(mine[s], 8, 0))
    low_end = [jnp.where(base[s] == 0, 0.0, 1.0) for s in range(slots)]
    high_end = [jnp.where(base[s] == 8, 0.0, 1.0) for s in range(slots)]
    emitted = set()
    value = {}

    def unpack(s):
        if ("u", s) not in emitted:
            emitted.add(("u", s))
            ready(s)
            flat[s, :, pl.ds(0, 16)] = feats_ref[s].astype(F32).reshape(128, 16, 128)

    def x_row(duo, q):
        if ("x", duo, q) in emitted:
            return
        emitted.add(("x", duo, q))
        for k in range(2):
            s = 2 * duo + k
            unpack(s)
            row = jnp.clip(base[s] - 2 + q, 0, 15)
            v = flat.at[s].reshape(128 * PITCH, 128)[pl.ds(row, 128, stride=PITCH), :]
            if q < 2:
                v = v * low_end[s]
            if q > 9:
                v = v * high_end[s]
            put_row(xbuf.at[duo], q, v, k * lanes)

    def before(op):
        kind, duo, q = op
        if kind == "hidden":
            for r in range(q, q + 4):
                x_row(duo, r)

    def product(op):
        kind, duo, q = op
        if kind == "hidden":
            big, data = big1, window(xbuf.at[duo], q, 4)
        else:
            big, data = big2, window(hbuf.at[duo], q, 4)
        value[op] = jnp.dot(big[...], data, preferred_element_type=F32)

    def after(op):
        kind, duo, q = op
        out = value.pop(op)
        if kind == "hidden":
            hid = out * sigmoid(out)
            for r in range(2):
                for k in range(2):
                    v = hid[r * 128 : (r + 1) * 128, k * lanes : (k + 1) * lanes]
                    if q + r == 0:
                        v = v * low_end[2 * duo + k]
                    if q + r == 9:
                        v = v * high_end[2 * duo + k]
                    put_row(hbuf.at[duo], q + r, v, k * lanes)
            return
        for k in range(2):
            s = 2 * duo + k
            live = jnp.where(s < count, 1.0, 0.0)
            keep = lane >= z0[s]
            for r in range(2):
                part = out[r * 64 : (r + 1) * 64, k * lanes : (k + 1) * lanes]
                weight = jnp.concatenate(
                    [
                        jnp.broadcast_to(
                            gauss_ref[x, pl.ds(base[s] + q + r, 1), :] * live, (16, lanes)
                        )
                        for x in range(4)
                    ],
                    axis=0,
                )
                turned = pltpu.roll(part * weight, lax.rem(z0[s], 128), 1)
                store(mine[s], q + r, jnp.where(keep, turned, 0.0), jnp.where(keep, 0.0, turned))

    order = []
    late = []
    for duo in range(slots // 2):
        for q in range(0, 10, 2):
            order.append(("hidden", duo, q))
            if late:
                order.append(late.pop(0))
        late = [("logits", duo, q) for q in range(0, 8, 2)]
    order += late
    before(order[0])
    before(order[1])
    for i, op in enumerate(order):
        product(op)
        if i > 0:
            after(order[i - 1])
        if i + 2 < len(order):
            before(order[i + 2])
    after(order[-1])


def outer_kernel(
    brick_s,
    z_s,
    count_s,
    feats_hbm,
    gauss_hbm,
    w1_hbm,
    w2_hbm,
    relayed,
    pair_ref,
    cross_ref,
    big1,
    big2,
    feats_ref,
    gauss_ref,
    w1_ref,
    w2_ref,
    flat,
    xbuf,
    hbuf,
    total,
    sems,
):
    slots = feats_ref.shape[0]
    copies = [
        pltpu.make_async_copy(w1_hbm, w1_ref, sems.at[slots]),
        pltpu.make_async_copy(w2_hbm, w2_ref, sems.at[slots + 1]),
        pltpu.make_async_copy(gauss_hbm, gauss_ref, sems.at[slots + 2]),
    ]
    for copy in copies:
        copy.start()
    loads = [
        pltpu.make_async_copy(feats_hbm.at[s], feats_ref.at[s], sems.at[s]) for s in range(slots)
    ]
    for load in loads:
        load.start()
    total[...] = jnp.zeros_like(total)
    for copy in copies:
        copy.wait()
    fill_big(big1, band(w1_ref, False), 2)
    fill_big(big2, band(w2_ref, True), 2)
    for load in loads:
        load.wait()

    def store(mine, row, low, high):
        side = jnp.where(mine, 1, 0)
        total[side, row, :, pl.ds(0, 128)] += low
        total[side, row, :, pl.ds(128, 128)] += high

    teacher_half(
        False,
        (brick_s, z_s, count_s),
        lambda s: None,
        feats_ref,
        gauss_ref,
        big1,
        big2,
        store,
        flat,
        xbuf,
        hbuf,
    )
    odd = parity()
    pair_ref[...] = total[1 - odd]
    cross_ref[...] = total[odd]


def own_kernel(
    brick_s,
    z_s,
    count_s,
    feats_ref,
    gauss_ref,
    big1,
    big2,
    pair_edge,
    cross_edge,
    own_ref,
    flat,
    xbuf,
    hbuf,
):
    own_ref[...] = jnp.zeros_like(own_ref)

    def store(mine, row, low, high):
        own_ref[row, :, pl.ds(0, 128)] += low
        own_ref[row, :, pl.ds(128, 128)] += high

    teacher_half(
        True,
        (brick_s, z_s, count_s),
        lambda s: None,
        feats_ref,
        gauss_ref,
        big1,
        big2,
        store,
        flat,
        xbuf,
        hbuf,
    )


SUMS = jax.ShapeDtypeStruct((8, 64, 256), F32)


def teacher_scratch(slots):
    return [
        pltpu.VMEM((slots, 128, PITCH, 128), F32),
        pltpu.VMEM((slots // 2, 3, 12, 128, 256), BF16),
        pltpu.VMEM((slots // 2, 3, 10, 128, 256), BF16),
    ]


def teacher_outer(brick, z, count, feats, gauss, w1, w2, relayed):
    slots = feats.shape[0]
    return pl.pallas_call(
        outer_kernel,
        name="teacher_outer",
        grid_spec=pltpu.PrefetchScalarGridSpec(
            num_scalar_prefetch=3,
            in_specs=[HBM] * 4 + [VMEM],
            out_specs=[VMEM] * 6,
            scratch_shapes=[pltpu.VMEM(w1.shape, BF16), pltpu.VMEM(w2.shape, BF16)]
            + teacher_scratch(slots)
            + [pltpu.VMEM((2, 8, 64, 256), F32), pltpu.SemaphoreType.DMA((slots + 3,))],
        ),
        out_shape=[
            SUMS,
            SUMS,
            jax.ShapeDtypeStruct((256, 1536), BF16),
            jax.ShapeDtypeStruct((128, 1536), BF16),
            jax.ShapeDtypeStruct(feats.shape, BF16),
            jax.ShapeDtypeStruct(gauss.shape, F32),
        ],
        compiler_params=params(28),
        cost_estimate=cost(5_000_000_000, 4_000_000),
    )(*map(in_hbm, (brick, z, count, feats, gauss, w1, w2)), relayed)


def teacher_own(brick, z, count, feats, gauss, big1, big2, pair, cross):
    return pl.pallas_call(
        own_kernel,
        name="teacher_own",
        grid_spec=pltpu.PrefetchScalarGridSpec(
            num_scalar_prefetch=3,
            in_specs=[VMEM] * 6,
            out_specs=VMEM,
            scratch_shapes=teacher_scratch(feats.shape[0]),
        ),
        out_shape=SUMS,
        compiler_params=params(28),
        cost_estimate=cost(4_000_000_000, 3_000_000),
    )(*map(in_hbm, (brick, z, count)), feats, gauss, big1, big2, pair, cross)


def relay_kernel(feats_hbm, main_ref, pair_ref, cross_ref, feats_ref, flat, sems):
    odd = parity()
    chunks = 4
    rows = 1024 // chunks
    loads = []
    for i in range(chunks):
        part = pl.ds(i * rows, rows)
        loads.append(pltpu.make_async_copy(feats_hbm.at[part], feats_ref.at[part], sems.at[i]))
        loads[i].start()
    for i in range(chunks):
        loads[i].wait()
        part = pl.ds(i * rows, rows)
        for h in range(2):
            flat[h, part] = feats_ref[part, pl.ds(h * 128, 128)].astype(F32)
            for y in range(8):
                main_ref[y, pl.ds(i * rows // 8, rows // 8), pl.ds(h * 128, 128)] = flat[
                    h, pl.ds(i * rows + y, rows // 8, stride=8), :
                ].astype(BF16)
    pair_ref[...] = main_ref[pl.ds(6 * (1 - odd), 2)]
    cross_ref[...] = main_ref[pl.ds(6 * odd, 2)]


def relay(feats):
    edge = jax.ShapeDtypeStruct((2, 128, 256), BF16)
    return pl.pallas_call(
        relay_kernel,
        name="relay",
        in_specs=[HBM],
        out_specs=[VMEM] * 3,
        out_shape=[jax.ShapeDtypeStruct((8, 128, 256), BF16), edge, edge],
        scratch_shapes=[
            pltpu.VMEM((1024, 256), BF16),
            pltpu.VMEM((2, 1024, 128), F32),
            pltpu.SemaphoreType.DMA((4,)),
        ],
        compiler_params=params(8),
        cost_estimate=cost(0, 1_500_000),
    )(in_hbm(feats))


def put_edges(store, pair_ref, cross_ref, low, high):
    odd = parity()
    for k in range(2):
        pair, cross = pair_ref[k].astype(F32), cross_ref[k].astype(F32)
        store(low + k, jnp.where(odd == 1, pair, cross))
        store(high + k, jnp.where(odd == 1, cross, pair))


def inside(y):
    position = lax.axis_index("gy")
    last = lax.axis_size("gy") - 1
    if y < 0:
        return jnp.where(position > 0, 1.0, 0.0)
    if y >= 8:
        return jnp.where(position < last, 1.0, 0.0)
    return None


def class_softmax(v):
    parts = []
    for x in range(4):
        block = v[x * 16 : (x + 1) * 16]
        peak = jnp.max(block, axis=0, keepdims=True)
        grown = jnp.exp(block - peak)
        parts.append(grown * (1.0 / jnp.sum(grown, axis=0, keepdims=True)))
    return jnp.concatenate(parts, axis=0)


def forward_kernel(
    main_ref, pair_ref, cross_ref, w1_ref, w2_ref, prob_ref, slope_ref, big1, big2, xbuf, hbuf
):
    fill_big(big1, band(w1_ref, False), 2)
    fill_big(big2, band(w2_ref, True), 2)
    store = lambda y, v: put_row(xbuf, y, v)
    put_edges(store, pair_ref, cross_ref, 0, 10)
    for y in range(2):
        store(y + 2, main_ref[y].astype(F32))
    for y in range(0, 10, 2):
        pre = jnp.dot(big1[...], window(xbuf, y, 4), preferred_element_type=F32)
        if y < 6:
            for k in range(2):
                store(y + k + 4, main_ref[y + k + 2].astype(F32))
        sig = sigmoid(pre)
        hid = pre * sig
        slope = sig * (1.0 + pre * (1.0 - sig))
        for k in range(2):
            row = y + k
            rows = slice(k * 128, (k + 1) * 128)
            slope_ref[row] = slope[rows]
            keep = inside(row - 1)
            put_row(hbuf, row, hid[rows] if keep is None else hid[rows] * keep)
    for y in range(0, 8, 2):
        logits = jnp.dot(big2[...], window(hbuf, y, 4), preferred_element_type=F32)
        for k in range(2):
            prob_ref[y + k] = class_softmax(logits[k * 64 : (k + 1) * 64])


def forward(main, pair, cross, w1, w2):
    return pl.pallas_call(
        forward_kernel,
        name="forward",
        in_specs=[VMEM] * 5,
        out_specs=[VMEM] * 2,
        out_shape=[SUMS, jax.ShapeDtypeStruct((10, 128, 256), F32)],
        scratch_shapes=[
            pltpu.VMEM((256, 1536), BF16),
            pltpu.VMEM((128, 1536), BF16),
            pltpu.VMEM((3, 12, 128, 256), BF16),
            pltpu.VMEM((3, 10, 128, 256), BF16),
        ],
        compiler_params=params(24),
        cost_estimate=cost(4_000_000_000, 3_000_000),
    )(main, pair, cross, w1, w2)


def combine_kernel(
    own_ref,
    from_pair_ref,
    from_cross_ref,
    prob_ref,
    sum_ref,
    main_ref,
    pair_ref,
    cross_ref,
    turn0,
    turn1,
):
    odd = parity()
    for y in range(8):
        value = own_ref[y] + from_pair_ref[y] + from_cross_ref[y]
        for x in range(4):
            for h, turn in enumerate((turn0, turn1)):
                turn[pl.ds(x * 8 + y, 16, stride=32), :] = value[
                    x * 16 : (x + 1) * 16, h * 128 : (h + 1) * 128
                ]
        main_ref[y] = (prob_ref[y] - class_softmax(value)).astype(BF16)
    pair_ref[...] = main_ref[pl.ds(6 * (1 - odd), 2)]
    cross_ref[...] = main_ref[pl.ds(6 * odd, 2)]
    sum_ref[:, pl.ds(0, 128)] = turn0[...]
    sum_ref[:, pl.ds(128, 128)] = turn1[...]


def combine(own, from_pair, from_cross, prob):
    edge = jax.ShapeDtypeStruct((2, 64, 256), BF16)
    return pl.pallas_call(
        combine_kernel,
        name="combine",
        in_specs=[VMEM] * 4,
        out_specs=[VMEM] * 4,
        out_shape=[
            jax.ShapeDtypeStruct((512, 256), F32),
            jax.ShapeDtypeStruct((8, 64, 256), BF16),
            edge,
            edge,
        ],
        scratch_shapes=[pltpu.VMEM((512, 128), F32)] * 2,
        compiler_params=params(8),
        cost_estimate=cost(1_000_000, 3_000_000),
    )(own, from_pair, from_cross, prob)


def put_out(turns, y, grad):
    for k in range(2):
        for x in range(4):
            for h, turn in enumerate(turns):
                at = k * 128 + x * 32
                turn[pl.ds(x * 8 + y + k, 32, stride=32), :] = grad[
                    at : at + 32, h * 128 : (h + 1) * 128
                ]


def inner_kernel(main_ref, slope_ref, w1_ref, w2_ref, turn0, turn1, pbuf, big1, big2, gbuf):
    flip2 = band(w2_ref, True)
    fill_big(big2, [flip2[8 - t].T for t in range(9)], 2)
    flip1 = band(w1_ref, True)
    fill_big(big1, [flip1[8 - t].T for t in range(9)], 2)
    for y in range(8):
        put_row(gbuf, y, main_ref[y].astype(F32))
    for y in range(0, 6, 2):
        grad = jnp.dot(big2[...], window(gbuf, y, 4), preferred_element_type=F32)
        for k in range(2):
            put_row(pbuf, y + k, grad[k * 128 : (k + 1) * 128] * slope_ref[y + k + 2])
    for y in range(0, 4, 2):
        grad = jnp.dot(big1[...], window(pbuf, y, 4), preferred_element_type=F32)
        put_out((turn0, turn1), y + 2, grad)


def inner(main, slope, w1, w2):
    turned = jax.ShapeDtypeStruct((1024, 128), F32)
    return pl.pallas_call(
        inner_kernel,
        name="inner",
        in_specs=[VMEM] * 4,
        out_specs=[VMEM] * 5,
        out_shape=[
            turned,
            turned,
            jax.ShapeDtypeStruct((3, 6, 128, 256), BF16),
            jax.ShapeDtypeStruct((256, 1536), BF16),
            jax.ShapeDtypeStruct((256, 768), BF16),
        ],
        scratch_shapes=[pltpu.VMEM((3, 8, 64, 256), BF16)],
        compiler_params=params(16),
        cost_estimate=cost(2_000_000_000, 3_000_000),
    )(main, slope, w1, w2)


def outer_rows_kernel(
    main_ref,
    pair_ref,
    cross_ref,
    slope_ref,
    done0,
    done1,
    pin_ref,
    big1,
    big2,
    out_ref,
    gbuf,
    pbuf,
    turn0,
    turn1,
):
    store = lambda y, v: put_row(gbuf, y, v)
    put_edges(store, pair_ref, cross_ref, 0, 6)
    for y, row in ((2, 0), (3, 1), (4, 6), (5, 7)):
        store(y, main_ref[row].astype(F32))
    for d in range(3):
        pbuf[d, pl.ds(2, 2)] = pin_ref[d, pl.ds(0, 2)]
        pbuf[d, pl.ds(4, 2)] = pin_ref[d, pl.ds(4, 2)]
    for g, p, row in ((0, 0, -1), (4, 6, 7)):
        grad = jnp.dot(big2[...], window(gbuf, g, 4), preferred_element_type=F32)
        for k in range(2):
            v = grad[k * 128 : (k + 1) * 128] * slope_ref[row + k + 1]
            keep = inside(row + k)
            put_row(pbuf, p + k, v if keep is None else v * keep)
    for p, row in ((0, 0), (4, 6)):
        grad = jnp.dot(big1[...], window(pbuf, p, 4), preferred_element_type=F32)
        put_out((turn0, turn1), row, grad)
    y = lax.broadcasted_iota(jnp.int32, (1024, 128), 0) % 8
    early = (y >= 2) & (y < 6)
    out_ref[:, pl.ds(0, 128)] = jnp.where(early, done0[...], turn0[...])
    out_ref[:, pl.ds(128, 128)] = jnp.where(early, done1[...], turn1[...])


def outer_rows(main, pair, cross, slope, done0, done1, pin, big1, big2):
    return pl.pallas_call(
        outer_rows_kernel,
        name="outer_rows",
        in_specs=[VMEM] * 9,
        out_specs=VMEM,
        out_shape=jax.ShapeDtypeStruct((1024, 256), F32),
        scratch_shapes=[
            pltpu.VMEM((3, 8, 64, 256), BF16),
            pltpu.VMEM((3, 8, 128, 256), BF16),
            pltpu.VMEM((1024, 128), F32),
            pltpu.VMEM((1024, 128), F32),
        ],
        compiler_params=params(16),
        cost_estimate=cost(2_000_000_000, 3_000_000),
    )(main, pair, cross, slope, done0, done1, pin, big1, big2)


def swap_pair(value):
    count = lax.axis_size("gy")
    return lax.ppermute(value, "gy", [(i, i ^ 1) for i in range(count)])


def swap_cross(value):
    count = lax.axis_size("gy")
    pairs = [(i, i + 1) for i in range(1, count - 1, 2)]
    return lax.ppermute(value, "gy", pairs + [(j, i) for i, j in pairs])


def taps_first(w):
    outs, ins = w.shape[:2]
    return jnp.transpose(w, (2, 3, 4, 0, 1)).reshape(3, 9, outs, ins)


def body(
    window_feats,
    window_brick,
    window_z,
    window_count,
    gaussian,
    brick_feats,
    teacher_w1,
    teacher_w2,
    student_w1,
    student_w2,
):
    tw1, tw2, sw1, sw2 = map(taps_first, (teacher_w1, teacher_w2, student_w1, student_w2))
    main, to_pair, to_cross = relay(brick_feats.reshape(1024, 256))
    edge_cross = swap_cross(to_cross)
    edge_pair = swap_pair(to_pair)
    feats = window_feats.reshape(window_feats.shape[0], 2048, 128)
    tables = (window_brick, window_z, window_count)
    sum_pair, sum_cross, *kept = teacher_outer(*tables, feats, gaussian, tw1, tw2, to_pair)
    got_cross = swap_cross(sum_cross)
    got_pair = swap_pair(sum_pair)
    big1, big2, held_feats, held_gauss = kept
    own = teacher_own(*tables, held_feats, held_gauss, big1, big2, edge_pair, edge_cross)
    prob, slope = forward(main, edge_pair, edge_cross, sw1, sw2)
    teacher_sum, grad, grad_pair, grad_cross = combine(own, got_pair, got_cross, prob)
    near_cross = swap_cross(grad_cross)
    near_pair = swap_pair(grad_pair)
    early = inner(grad, slope, sw1, sw2)
    feature_grad = outer_rows(grad, near_pair, near_cross, slope, *early)
    return (teacher_sum.reshape(16, 4, 8, 256), feature_grad.reshape(32, 4, 8, 256))


def solution(mesh):
    placed = (
        P(("grp", "gy"), None, None, None, None),
        P("grp"),
        P("grp"),
        P("grp"),
        P(),
        P(None, None, ("grp", "gy"), None),
        P(),
        P(),
        P(),
        P(),
    )
    return jax.shard_map(
        body,
        mesh=mesh,
        in_specs=placed,
        out_specs=(P(None, None, ("grp", "gy"), None), P(None, None, ("grp", "gy"), None)),
        check_vma=False,
    )
```

time: 57.4 us -> 40.4 us (0.70)
  the two profiles are of different devices: /device:TPU:7 before, /device:TPU:1 now
where the time goes in v1:
time: 40.4 us; the launch traced here: 39.6 us
  Pallas kernels  22.1 us (55%)
  starting transfers between devices  12.8 us (32%)
  waiting for transfers between devices  3.97 us (10%)
  between operations  0.77 us (2%)
    ppermute x3, starting transfers between devices, swap_cross(): return lax.ppermute(value, 'gy', pairs + [(j, i) for i, j in pairs])  12.6 us
    pallas_call x1, Pallas kernels, teacher_outer(): pl.pallas_call(outer_kernel, name='teacher_outer', grid_spec=pltpu.Prefet...  7.15 us
    pallas_call x1, Pallas kernels, teacher_own(): pl.pallas_call(own_kernel, name='teacher_own', grid_spec=pltpu.PrefetchSc...  5.08 us
    ppermute x3, waiting for transfers between devices, swap_cross(): return lax.ppermute(value, 'gy', pairs + [(j, i) for i, j in pairs])  3.97 us
    pallas_call x1, Pallas kernels, outer_rows(): pl.pallas_call(outer_rows_kernel, name='outer_rows', in_specs=[VMEM] * 9,...  2.59 us
    pallas_call x1, Pallas kernels, forward(): pl.pallas_call(forward_kernel, name='forward', in_specs=[VMEM] * 5, out_s...  2.44 us
    pallas_call x1, Pallas kernels, inner(): pl.pallas_call(inner_kernel, name='inner', in_specs=[VMEM] * 4, out_specs...  2.07 us
    pallas_call x1, Pallas kernels, combine(): pl.pallas_call(combine_kernel, name='combine', in_specs=[VMEM] * 4, out_s...  1.51 us
  transfers between devices with their start and end apart: 6, of which 1 were waited for; matrix products, arithmetic and copies ran while one was open for 0% of the time, Pallas kernels for 42%

profile of v1, /device:TPU:1, one launch (start us, length us, event | category | flops | bytes accessed | tf_op | source)
XLA Modules:
  0.0 39.6 jit_solution(17355522055334523673)
XLA Ops:
  0.6 1.2 %relay.1 = (bf16[8,128,256]{2,1,0:T(8,128)(2,1)S(1)}, bf16[2,128,256]{2,1,0:T(8,128)(2,1)S(1)}, bf16[2,128,256]{2,1,0:T(8,128)(2,1)S(1)}) custom-call(bf16[1024,256]{1,0:T(8,128)(2,1)} %bitcast.20), custom_call_target="tpu_custom_call" | custom-call | bytes 1500000 | tf_op jit(solution)/shard_map/relay/pallas_call | solution.py:393
  1.9 0.1 collective-permute-start
  2.0 4.5 %collective-permute-start.1 = (bf16[2,128,256]{2,1,0:T(8,128)(2,1)S(1)}, bf16[2,128,256]{2,1,0:T(8,128)(2,1)S(1)}, u32[]{:S(2)}, u32[]{:S(2)}) collective-permute-start(bf16[2,128,256]{2,1,0:T(8,128)(2,1)S(1)} %get-tuple-element.27), channel_id=1, source_target_pairs={{1,2},{3,4},{5,6},{7,8},{9,10},{11,12},{13,14},{2,1},{4,3},{6,5},{... | collective-permute-start | bytes 393224 | tf_op jit(solution)/shard_map/ppermute | solution.py:640
  6.5 0.0 copy-start
  6.5 0.0 copy-start.1
  6.5 7.2 %teacher_outer.1 = (f32[8,64,256]{2,1,0:T(8,128)S(1)}, f32[8,64,256]{2,1,0:T(8,128)S(1)}, bf16[256,1536]{1,0:T(8,128)(2,1)S(1)}, bf16[128,1536]{1,0:T(8,128)(2,1...) custom-call(s32[64]{0:T(128)} %brick_s.3, s32[64]{0:T(128)} %z_s.3, s32[16]{0:T(128)} %count_s.3, ...), custom_call_target="tpu_custom_call" | custom-call | flops 5000000000 | bytes 4000000 | tf_op jit(solution)/shard_map/teacher_outer/pallas_call | solution.py:329
  13.7 0.1 collective-permute-start.2
  13.8 3.7 %collective-permute-start.3 = (f32[8,64,256]{2,1,0:T(8,128)S(1)}, f32[8,64,256]{2,1,0:T(8,128)S(1)}, u32[]{:S(2)}, u32[]{:S(2)}) collective-permute-start(f32[8,64,256]{2,1,0:T(8,128)S(1)} %get-tuple-element.29), channel_id=1, source_target_pairs={{1,2},{3,4},{5,6},{7,8},{9,10},{11,12},{13,14},{2,1},{4,3},{6,5},{... | collective-permute-start | bytes 1572872 | tf_op jit(solution)/shard_map/ppermute | solution.py:640
  17.4 0.0 collective-permute-done.pair_edge.pair_ref
  17.5 0.0 collective-permute-done.1.cross_edge.cross_ref
  17.5 0.0 copy-done
  17.5 0.0 copy-done.1
  17.5 2.4 %forward.1 = (f32[8,64,256]{2,1,0:T(8,128)S(1)}, f32[10,128,256]{2,1,0:T(8,128)S(1)}) custom-call(bf16[8,128,256]{2,1,0:T(8,128)(2,1)S(1)} %get-tuple-element.30.main_ref, bf16[2,128,256]{2,1,0:T(8,128)(2,1)S(1)} %collective-permute-done.pair_edge.pair_ref, bf16[2,128,256]{2,1,0:T(8,128)(2,1)S(1)} %collective-permute-done.1.cross_edge.cross_ref, ...), custom_call_target="tpu_custom_call" | custom-call | flops 4000000000 | bytes 3000000 | tf_op jit(solution)/shard_map/forward/pallas_call | solution.py:467
  19.9 5.1 %teacher_own.1.own_ref = f32[8,64,256]{2,1,0:T(8,128)S(1)} custom-call(s32[64]{0:T(128)} %brick_s.3, s32[64]{0:T(128)} %z_s.3, s32[16]{0:T(128)} %count_s.3, bf16[4,2048,128]{2,1,0:T(8,128)(2,1)S(1)} %get-tuple-element.23.feats_ref, f32[4,16,128]{2,1,0:T(8,128)S(1)} %get-tuple-element.24.gauss_ref, bf16[256,1536]{1,0:T(8,128)(2,1)S(1)} %get-tuple-element.25.big1, ...), custom_call_target="tpu_custom_call" | custom-call | flops 4000000000 | bytes 3000000 | tf_op jit(solution)/shard_map/teacher_own/pallas_call | solution.py:354
  25.0 0.0 collective-permute-done.2.from_pair_ref
  25.0 4.0 %collective-permute-done.3.from_cross_ref = f32[8,64,256]{2,1,0:T(8,128)S(1)} collective-permute-done((f32[8,64,256]{2,1,0:T(8,128)S(1)}, f32[8,64,256]{2,1,0:T(8,128)S(1)}, u32[]{:S(2)}, u32[]{:S(2)}) %collective-permute-start.3) | collective-permute-done | bytes 524320 | tf_op jit(solution)/shard_map/ppermute | solution.py:640
  29.0 1.5 %combine.1 = (f32[512,256]{1,0:T(8,128)}, bf16[8,64,256]{2,1,0:T(8,128)(2,1)S(1)}, bf16[2,64,256]{2,1,0:T(8,128)(2,1)S(1)}, bf16[2,64,256]{2,1,0:T(8,128)(2,1)S(1)}) custom-call(f32[8,64,256]{2,1,0:T(8,128)S(1)} %teacher_own.1.own_ref, f32[8,64,256]{2,1,0:T(8,128)S(1)} %collective-permute-done.2.from_pair_ref, ...), custom_call_target="tpu_custom_call" | custom-call | flops 1000000 | bytes 3000000 | tf_op jit(solution)/shard_map/combine/pallas_call | solution.py:513
  30.5 0.0 collective-permute-start.4
  30.5 4.4 %collective-permute-start.5 = (bf16[2,64,256]{2,1,0:T(8,128)(2,1)S(1)}, bf16[2,64,256]{2,1,0:T(8,128)(2,1)S(1)}, u32[]{:S(2)}, u32[]{:S(2)}) collective-permute-start(bf16[2,64,256]{2,1,0:T(8,128)(2,1)S(1)} %get-tuple-element.35), channel_id=1, source_target_pairs={{1,2},{3,4},{5,6},{7,8},{9,10},{11,12},{13,14},{2,1},{4,3},{6,5},{... | collective-permute-start | bytes 196616 | tf_op jit(solution)/shard_map/ppermute | solution.py:640
  34.9 2.1 %inner.1 = (f32[1024,128]{1,0:T(8,128)S(1)}, f32[1024,128]{1,0:T(8,128)S(1)}, bf16[3,6,128,256]{3,2,1,0:T(8,128)(2,1)S(1)}, bf16[256,1536]{1,0:T(8,128)(2,1)S(1)}, bf16[256,768]{1,0:T(8,128)(2,1)S(1)}) custom-call(bf16[8,64,256]{2,1,0:T(8,128)(2,1)S(1)} %get-tuple-element.33.main_ref, f32[10,128,256]{2,1,0:T(8,128)S(1)} %get-tuple-element.36.slope_ref, ...), custom_call_target="tpu_custom_call" | custom-call | flops 2000000000 | bytes 3000000 | tf_op jit(solution)/shard_map/inner/pallas_call | solution.py:558
  37.0 0.0 collective-permute-done.4.pair_ref
  37.0 0.0 collective-permute-done.5.cross_ref
  37.0 2.6 %outer_rows.1 = f32[1024,256]{1,0:T(8,128)} custom-call(bf16[8,64,256]{2,1,0:T(8,128)(2,1)S(1)} %get-tuple-element.33.main_ref, bf16[2,64,256]{2,1,0:T(8,128)(2,1)S(1)} %collective-permute-done.4.pair_ref, bf16[2,64,256]{2,1,0:T(8,128)(2,1)S(1)} %collective-permute-done.5.cross_ref, f32[10,128,256]{2,1,0:T(8,128)S(1)} %get-tuple-element.36.slope_ref, ...), custom_call_target="tpu_custom_call" | custom-call | flops 2000000000 | bytes 3000000 | tf_op jit(solution)/shard_map/outer_rows/pallas_call | solution.py:615
Async XLA Ops:
  1.9 15.6 %collective-permute-start = (bf16[2,128,256]{2,1,0:T(8,128)(2,1)S(1)}, bf16[2,128,256]{2,1,0:T(8,128)(2,1)S(1)}, u32[]{:S(2)}, u32[]{:S(2)}) collective-permute-start(bf16[2,128,256]{2,1,0:T(8,128)(2,1)S(1)} %get-tuple-element.22.relayed), channel_id=1, source_target_pairs={{0,1},{1,0},{2,3},{3,2},{4,5},{5,4},{6,7},{7,6},{8,9},{9,8},{10,11... | collective-permute-start | bytes 393224 | tf_op jit(solution)/shard_map/ppermute | solution.py:634
  2.0 15.5 %collective-permute-start.1 = (bf16[2,128,256]{2,1,0:T(8,128)(2,1)S(1)}, bf16[2,128,256]{2,1,0:T(8,128)(2,1)S(1)}, u32[]{:S(2)}, u32[]{:S(2)}) collective-permute-start(bf16[2,128,256]{2,1,0:T(8,128)(2,1)S(1)} %get-tuple-element.27), channel_id=1, source_target_pairs={{1,2},{3,4},{5,6},{7,8},{9,10},{11,12},{13,14},{2,1},{4,3},{6,5},{... | collective-permute-start | bytes 393224 | tf_op jit(solution)/shard_map/ppermute | solution.py:640
  6.5 11.0 %copy-start = (bf16[32,32,3,3,3]{1,0,4,3,2:T(8,128)(2,1)S(1)}, bf16[32,32,3,3,3]{1,0,4,3,2:T(8,128)(2,1)}, u32[]{:S(2)}) copy-start(bf16[32,32,3,3,3]{1,0,4,3,2:T(8,128)(2,1)} %param.18) | copy-start | bytes 165892
  6.5 11.0 %copy-start.1 = (bf16[16,32,3,3,3]{1,0,4,3,2:T(8,128)(2,1)S(1)}, bf16[16,32,3,3,3]{1,0,4,3,2:T(8,128)(2,1)}, u32[]{:S(2)}) copy-start(bf16[16,32,3,3,3]{1,0,4,3,2:T(8,128)(2,1)} %param.19) | copy-start | bytes 82948
  13.7 11.3 %collective-permute-start.2 = (f32[8,64,256]{2,1,0:T(8,128)S(1)}, f32[8,64,256]{2,1,0:T(8,128)S(1)}, u32[]{:S(2)}, u32[]{:S(2)}) collective-permute-start(f32[8,64,256]{2,1,0:T(8,128)S(1)} %get-tuple-element.28), channel_id=1, source_target_pairs={{0,1},{1,0},{2,3},{3,2},{4,5},{5,4},{6,7},{7,6},{8,9},{9,8},{10,11... | collective-permute-start | bytes 1572872 | tf_op jit(solution)/shard_map/ppermute | solution.py:634
  13.8 15.2 %collective-permute-start.3 = (f32[8,64,256]{2,1,0:T(8,128)S(1)}, f32[8,64,256]{2,1,0:T(8,128)S(1)}, u32[]{:S(2)}, u32[]{:S(2)}) collective-permute-start(f32[8,64,256]{2,1,0:T(8,128)S(1)} %get-tuple-element.29), channel_id=1, source_target_pairs={{1,2},{3,4},{5,6},{7,8},{9,10},{11,12},{13,14},{2,1},{4,3},{6,5},{... | collective-permute-start | bytes 1572872 | tf_op jit(solution)/shard_map/ppermute | solution.py:640
  30.5 6.5 %collective-permute-start.4 = (bf16[2,64,256]{2,1,0:T(8,128)(2,1)S(1)}, bf16[2,64,256]{2,1,0:T(8,128)(2,1)S(1)}, u32[]{:S(2)}, u32[]{:S(2)}) collective-permute-start(bf16[2,64,256]{2,1,0:T(8,128)(2,1)S(1)} %get-tuple-element.34), channel_id=1, source_target_pairs={{0,1},{1,0},{2,3},{3,2},{4,5},{5,4},{6,7},{7,6},{8,9},{9,8},{10,11... | collective-permute-start | bytes 196616 | tf_op jit(solution)/shard_map/ppermute | solution.py:634
  30.5 6.5 %collective-permute-start.5 = (bf16[2,64,256]{2,1,0:T(8,128)(2,1)S(1)}, bf16[2,64,256]{2,1,0:T(8,128)(2,1)S(1)}, u32[]{:S(2)}, u32[]{:S(2)}) collective-permute-start(bf16[2,64,256]{2,1,0:T(8,128)(2,1)S(1)} %get-tuple-element.35), channel_id=1, source_target_pairs={{1,2},{3,4},{5,6},{7,8},{9,10},{11,12},{13,14},{2,1},{4,3},{6,5},{... | collective-permute-start | bytes 196616 | tf_op jit(solution)/shard_map/ppermute | solution.py:640

commit v2 on v1

--- a/solution.py
+++ b/solution.py
@@ -218,7 +218,6 @@
     gauss_hbm,
     w1_hbm,
     w2_hbm,
-    relayed,
     pair_ref,
     cross_ref,
     big1,
@@ -251,8 +250,6 @@
         copy.wait()
     fill_big(big1, band(w1_ref, False), 2)
     fill_big(big2, band(w2_ref, True), 2)
-    for load in loads:
-        load.wait()
 
     def store(mine, row, low, high):
         side = jnp.where(mine, 1, 0)
@@ -262,7 +259,7 @@
     teacher_half(
         False,
         (brick_s, z_s, count_s),
-        lambda s: None,
+        lambda s: loads[s].wait(),
         feats_ref,
         gauss_ref,
         big1,
@@ -285,8 +282,6 @@
     gauss_ref,
     big1,
     big2,
-    pair_edge,
-    cross_edge,
     own_ref,
     flat,
     xbuf,
@@ -324,14 +319,14 @@
     ]
 
 
-def teacher_outer(brick, z, count, feats, gauss, w1, w2, relayed):
+def teacher_outer(brick, z, count, feats, gauss, w1, w2):
     slots = feats.shape[0]
     return pl.pallas_call(
         outer_kernel,
         name="teacher_outer",
         grid_spec=pltpu.PrefetchScalarGridSpec(
             num_scalar_prefetch=3,
-            in_specs=[HBM] * 4 + [VMEM],
+            in_specs=[HBM] * 4,
             out_specs=[VMEM] * 6,
             scratch_shapes=[pltpu.VMEM(w1.shape, BF16), pltpu.VMEM(w2.shape, BF16)]
             + teacher_scratch(slots)
@@ -347,26 +342,26 @@
         ],
         compiler_params=params(28),
         cost_estimate=cost(5_000_000_000, 4_000_000),
-    )(*map(in_hbm, (brick, z, count, feats, gauss, w1, w2)), relayed)
-
-
-def teacher_own(brick, z, count, feats, gauss, big1, big2, pair, cross):
+    )(*map(in_hbm, (brick, z, count, feats, gauss, w1, w2)))
+
+
+def teacher_own(brick, z, count, feats, gauss, big1, big2):
     return pl.pallas_call(
         own_kernel,
         name="teacher_own",
         grid_spec=pltpu.PrefetchScalarGridSpec(
             num_scalar_prefetch=3,
-            in_specs=[VMEM] * 6,
+            in_specs=[VMEM] * 4,
             out_specs=VMEM,
             scratch_shapes=teacher_scratch(feats.shape[0]),
         ),
         out_shape=SUMS,
         compiler_params=params(28),
         cost_estimate=cost(4_000_000_000, 3_000_000),
-    )(*map(in_hbm, (brick, z, count)), feats, gauss, big1, big2, pair, cross)
-
-
-def relay_kernel(feats_hbm, main_ref, pair_ref, cross_ref, feats_ref, flat, sems):
+    )(*map(in_hbm, (brick, z, count)), feats, gauss, big1, big2)
+
+
+def relay_kernel(feats_hbm, behind, main_ref, pair_ref, cross_ref, feats_ref, flat, sems):
     odd = parity()
     chunks = 4
     rows = 1024 // chunks
@@ -388,12 +383,12 @@
     cross_ref[...] = main_ref[pl.ds(6 * odd, 2)]
 
 
-def relay(feats):
+def relay(feats, behind):
     edge = jax.ShapeDtypeStruct((2, 128, 256), BF16)
     return pl.pallas_call(
         relay_kernel,
         name="relay",
-        in_specs=[HBM],
+        in_specs=[HBM, VMEM],
         out_specs=[VMEM] * 3,
         out_shape=[jax.ShapeDtypeStruct((8, 128, 256), BF16), edge, edge],
         scratch_shapes=[
@@ -403,7 +398,7 @@
         ],
         compiler_params=params(8),
         cost_estimate=cost(0, 1_500_000),
-    )(in_hbm(feats))
+    )(in_hbm(feats), behind)
 
 
 def put_edges(store, pair_ref, cross_ref, low, high):
@@ -434,97 +429,114 @@
     return jnp.concatenate(parts, axis=0)
 
 
-def forward_kernel(
-    main_ref, pair_ref, cross_ref, w1_ref, w2_ref, prob_ref, slope_ref, big1, big2, xbuf, hbuf
-):
+def activate(pre):
+    sig = sigmoid(pre)
+    return pre * sig, sig * (1.0 + pre * (1.0 - sig))
+
+
+def forward_kernel(main_ref, w1_ref, w2_ref, prob_ref, slope_ref, hbuf, big1, big2, xbuf):
     fill_big(big1, band(w1_ref, False), 2)
     fill_big(big2, band(w2_ref, True), 2)
-    store = lambda y, v: put_row(xbuf, y, v)
-    put_edges(store, pair_ref, cross_ref, 0, 10)
-    for y in range(2):
-        store(y + 2, main_ref[y].astype(F32))
-    for y in range(0, 10, 2):
+    for y in range(4):
+        put_row(xbuf, y, main_ref[y].astype(F32))
+    for y in range(0, 6, 2):
         pre = jnp.dot(big1[...], window(xbuf, y, 4), preferred_element_type=F32)
-        if y < 6:
-            for k in range(2):
-                store(y + k + 4, main_ref[y + k + 2].astype(F32))
-        sig = sigmoid(pre)
-        hid = pre * sig
-        slope = sig * (1.0 + pre * (1.0 - sig))
+        if y < 4:
+            for k in range(4, 6):
+                put_row(xbuf, y + k, main_ref[y + k].astype(F32))
+        hid, slope = activate(pre)
         for k in range(2):
-            row = y + k
             rows = slice(k * 128, (k + 1) * 128)
-            slope_ref[row] = slope[rows]
-            keep = inside(row - 1)
-            put_row(hbuf, row, hid[rows] if keep is None else hid[rows] * keep)
-    for y in range(0, 8, 2):
+            slope_ref[y + k] = slope[rows]
+            put_row(hbuf, y + k, hid[rows])
+    for y in range(0, 4, 2):
         logits = jnp.dot(big2[...], window(hbuf, y, 4), preferred_element_type=F32)
         for k in range(2):
             prob_ref[y + k] = class_softmax(logits[k * 64 : (k + 1) * 64])
 
 
-def forward(main, pair, cross, w1, w2):
+def forward(main, w1, w2):
     return pl.pallas_call(
         forward_kernel,
         name="forward",
-        in_specs=[VMEM] * 5,
-        out_specs=[VMEM] * 2,
-        out_shape=[SUMS, jax.ShapeDtypeStruct((10, 128, 256), F32)],
-        scratch_shapes=[
-            pltpu.VMEM((256, 1536), BF16),
-            pltpu.VMEM((128, 1536), BF16),
-            pltpu.VMEM((3, 12, 128, 256), BF16),
-            pltpu.VMEM((3, 10, 128, 256), BF16),
+        in_specs=[VMEM] * 3,
+        out_specs=[VMEM] * 5,
+        out_shape=[
+            jax.ShapeDtypeStruct((4, 64, 256), F32),
+            jax.ShapeDtypeStruct((6, 128, 256), F32),
+            jax.ShapeDtypeStruct((3, 6, 128, 256), BF16),
+            jax.ShapeDtypeStruct((256, 1536), BF16),
+            jax.ShapeDtypeStruct((128, 1536), BF16),
         ],
-        compiler_params=params(24),
+        scratch_shapes=[pltpu.VMEM((3, 8, 128, 256), BF16)],
+        compiler_params=params(16),
         cost_estimate=cost(4_000_000_000, 3_000_000),
-    )(main, pair, cross, w1, w2)
-
-
-def combine_kernel(
+    )(main, w1, w2)
+
+
+def edge_kernel(
+    main_ref,
+    pair_in,
+    cross_in,
+    hin_ref,
+    big1,
+    big2,
     own_ref,
     from_pair_ref,
     from_cross_ref,
-    prob_ref,
-    sum_ref,
-    main_ref,
     pair_ref,
     cross_ref,
-    turn0,
-    turn1,
+    grad_ref,
+    slope_ref,
+    xbuf,
+    hbuf,
 ):
+    put_edges(lambda y, v: put_row(xbuf, y, v), pair_in, cross_in, 0, 6)
+    for y, row in ((2, 0), (3, 1), (4, 6), (5, 7)):
+        put_row(xbuf, y, main_ref[row].astype(F32))
+    for d in range(3):
+        hbuf[d, pl.ds(2, 2)] = hin_ref[d, pl.ds(0, 2)]
+        hbuf[d, pl.ds(4, 2)] = hin_ref[d, pl.ds(4, 2)]
+    for g, h, row in ((0, 0, -1), (4, 6, 7)):
+        pre = jnp.dot(big1[...], window(xbuf, g, 4), preferred_element_type=F32)
+        hid, slope = activate(pre)
+        for k in range(2):
+            rows = slice(k * 128, (k + 1) * 128)
+            slope_ref[g // 2 + k] = slope[rows]
+            keep = inside(row + k)
+            put_row(hbuf, h + k, hid[rows] if keep is None else hid[rows] * keep)
+    for g, row in ((0, 0), (4, 6)):
+        logits = jnp.dot(big2[...], window(hbuf, g, 4), preferred_element_type=F32)
+        for k in range(2):
+            y = row + k
+            value = own_ref[y] + from_pair_ref[y] + from_cross_ref[y]
+            prob = class_softmax(logits[k * 64 : (k + 1) * 64])
+            grad_ref[g // 2 + k] = (prob - class_softmax(value)).astype(BF16)
     odd = parity()
-    for y in range(8):
-        value = own_ref[y] + from_pair_ref[y] + from_cross_ref[y]
-        for x in range(4):
-            for h, turn in enumerate((turn0, turn1)):
-                turn[pl.ds(x * 8 + y, 16, stride=32), :] = value[
-                    x * 16 : (x + 1) * 16, h * 128 : (h + 1) * 128
-                ]
-        main_ref[y] = (prob_ref[y] - class_softmax(value)).astype(BF16)
-    pair_ref[...] = main_ref[pl.ds(6 * (1 - odd), 2)]
-    cross_ref[...] = main_ref[pl.ds(6 * odd, 2)]
-    sum_ref[:, pl.ds(0, 128)] = turn0[...]
-    sum_ref[:, pl.ds(128, 128)] = turn1[...]
-
-
-def combine(own, from_pair, from_cross, prob):
+    pair_ref[...] = grad_ref[pl.ds(2 * (1 - odd), 2)]
+    cross_ref[...] = grad_ref[pl.ds(2 * odd, 2)]
+
+
+def edge_grads(main, pair, cross, hidden, big1, big2, own, from_pair, from_cross):
     edge = jax.ShapeDtypeStruct((2, 64, 256), BF16)
     return pl.pallas_call(
-        combine_kernel,
-        name="combine",
-        in_specs=[VMEM] * 4,
+        edge_kernel,
+        name="edge_grads",
+        in_specs=[VMEM] * 9,
         out_specs=[VMEM] * 4,
         out_shape=[
-            jax.ShapeDtypeStruct((512, 256), F32),
-            jax.ShapeDtypeStruct((8, 64, 256), BF16),
             edge,
             edge,
+            jax.ShapeDtypeStruct((4, 64, 256), BF16),
+            jax.ShapeDtypeStruct((4, 128, 256), F32),
         ],
-        scratch_shapes=[pltpu.VMEM((512, 128), F32)] * 2,
-        compiler_params=params(8),
-        cost_estimate=cost(1_000_000, 3_000_000),
-    )(own, from_pair, from_cross, prob)
+        scratch_shapes=[
+            pltpu.VMEM((3, 8, 128, 256), BF16),
+            pltpu.VMEM((3, 8, 128, 256), BF16),
+        ],
+        compiler_params=params(12),
+        cost_estimate=cost(2_000_000_000, 3_000_000),
+    )(main, pair, cross, hidden, big1, big2, own, from_pair, from_cross)
 
 
 def put_out(turns, y, grad):
@@ -537,40 +549,82 @@
                 ]
 
 
-def inner_kernel(main_ref, slope_ref, w1_ref, w2_ref, turn0, turn1, pbuf, big1, big2, gbuf):
+def inner_kernel(
+    own_ref,
+    from_pair_ref,
+    from_cross_ref,
+    prob_ref,
+    grad_ref,
+    slope_ref,
+    w1_ref,
+    w2_ref,
+    sum_hbm,
+    turn0,
+    turn1,
+    pbuf,
+    big1,
+    big2,
+    gbuf,
+    sum0,
+    sum1,
+    sum_ref,
+    sem,
+):
+    for y in range(8):
+        value = own_ref[y] + from_pair_ref[y] + from_cross_ref[y]
+        for x in range(4):
+            for h, turn in enumerate((sum0, sum1)):
+                turn[pl.ds(x * 8 + y, 16, stride=32), :] = value[
+                    x * 16 : (x + 1) * 16, h * 128 : (h + 1) * 128
+                ]
+        if 2 <= y < 6:
+            grad = (prob_ref[y - 2] - class_softmax(value)).astype(BF16)
+        else:
+            grad = grad_ref[y if y < 2 else y - 4]
+        put_row(gbuf, y, grad.astype(F32))
+    sum_ref[:, pl.ds(0, 128)] = sum0[...]
+    sum_ref[:, pl.ds(128, 128)] = sum1[...]
+    copy = pltpu.make_async_copy(sum_ref, sum_hbm, sem)
+    copy.start()
     flip2 = band(w2_ref, True)
     fill_big(big2, [flip2[8 - t].T for t in range(9)], 2)
     flip1 = band(w1_ref, True)
     fill_big(big1, [flip1[8 - t].T for t in range(9)], 2)
-    for y in range(8):
-        put_row(gbuf, y, main_ref[y].astype(F32))
     for y in range(0, 6, 2):
         grad = jnp.dot(big2[...], window(gbuf, y, 4), preferred_element_type=F32)
         for k in range(2):
-            put_row(pbuf, y + k, grad[k * 128 : (k + 1) * 128] * slope_ref[y + k + 2])
+            put_row(pbuf, y + k, grad[k * 128 : (k + 1) * 128] * slope_ref[y + k])
     for y in range(0, 4, 2):
         grad = jnp.dot(big1[...], window(pbuf, y, 4), preferred_element_type=F32)
         put_out((turn0, turn1), y + 2, grad)
-
-
-def inner(main, slope, w1, w2):
+    copy.wait()
+
+
+def inner(own, from_pair, from_cross, prob, grad, slope, w1, w2):
     turned = jax.ShapeDtypeStruct((1024, 128), F32)
     return pl.pallas_call(
         inner_kernel,
         name="inner",
-        in_specs=[VMEM] * 4,
-        out_specs=[VMEM] * 5,
+        in_specs=[VMEM] * 8,
+        out_specs=[HBM] + [VMEM] * 5,
         out_shape=[
+            jax.ShapeDtypeStruct((512, 256), F32),
             turned,
             turned,
             jax.ShapeDtypeStruct((3, 6, 128, 256), BF16),
             jax.ShapeDtypeStruct((256, 1536), BF16),
             jax.ShapeDtypeStruct((256, 768), BF16),
         ],
-        scratch_shapes=[pltpu.VMEM((3, 8, 64, 256), BF16)],
+        scratch_shapes=[
+            pltpu.VMEM((3, 8, 64, 256), BF16),
+            pltpu.VMEM((512, 128), F32),
+            pltpu.VMEM((512, 128), F32),
+            pltpu.VMEM((512, 256), F32),
+            pltpu.SemaphoreType.DMA,
+        ],
         compiler_params=params(16),
-        cost_estimate=cost(2_000_000_000, 3_000_000),
-    )(main, slope, w1, w2)
+        cost_estimate=cost(4_000_000_000, 3_000_000),
+    )(own, from_pair, from_cross, prob, grad, slope, w1, w2)
 
 
 def outer_rows_kernel(
@@ -583,32 +637,43 @@
     pin_ref,
     big1,
     big2,
-    out_ref,
+    out_hbm,
     gbuf,
     pbuf,
     turn0,
     turn1,
+    out_ref,
+    sems,
 ):
     store = lambda y, v: put_row(gbuf, y, v)
     put_edges(store, pair_ref, cross_ref, 0, 6)
-    for y, row in ((2, 0), (3, 1), (4, 6), (5, 7)):
-        store(y, main_ref[row].astype(F32))
+    for y in range(4):
+        store(y + 2, main_ref[y].astype(F32))
     for d in range(3):
         pbuf[d, pl.ds(2, 2)] = pin_ref[d, pl.ds(0, 2)]
         pbuf[d, pl.ds(4, 2)] = pin_ref[d, pl.ds(4, 2)]
     for g, p, row in ((0, 0, -1), (4, 6, 7)):
         grad = jnp.dot(big2[...], window(gbuf, g, 4), preferred_element_type=F32)
         for k in range(2):
-            v = grad[k * 128 : (k + 1) * 128] * slope_ref[row + k + 1]
+            v = grad[k * 128 : (k + 1) * 128] * slope_ref[g // 2 + k]
             keep = inside(row + k)
             put_row(pbuf, p + k, v if keep is None else v * keep)
     for p, row in ((0, 0), (4, 6)):
         grad = jnp.dot(big1[...], window(pbuf, p, 4), preferred_element_type=F32)
         put_out((turn0, turn1), row, grad)
-    y = lax.broadcasted_iota(jnp.int32, (1024, 128), 0) % 8
+    chunks = 4
+    rows = 1024 // chunks
+    y = lax.broadcasted_iota(jnp.int32, (rows, 128), 0) % 8
     early = (y >= 2) & (y < 6)
-    out_ref[:, pl.ds(0, 128)] = jnp.where(early, done0[...], turn0[...])
-    out_ref[:, pl.ds(128, 128)] = jnp.where(early, done1[...], turn1[...])
+    copies = []
+    for i in range(chunks):
+        part = pl.ds(i * rows, rows)
+        out_ref[part, pl.ds(0, 128)] = jnp.where(early, done0[part], turn0[part])
+        out_ref[part, pl.ds(128, 128)] = jnp.where(early, done1[part], turn1[part])
+        copies.append(pltpu.make_async_copy(out_ref.at[part], out_hbm.at[part], sems.at[i]))
+        copies[i].start()
+    for copy in copies:
+        copy.wait()
 
 
 def outer_rows(main, pair, cross, slope, done0, done1, pin, big1, big2):
@@ -616,13 +681,15 @@
         outer_rows_kernel,
         name="outer_rows",
         in_specs=[VMEM] * 9,
-        out_specs=VMEM,
+        out_specs=HBM,
         out_shape=jax.ShapeDtypeStruct((1024, 256), F32),
         scratch_shapes=[
             pltpu.VMEM((3, 8, 64, 256), BF16),
             pltpu.VMEM((3, 8, 128, 256), BF16),
             pltpu.VMEM((1024, 128), F32),
             pltpu.VMEM((1024, 128), F32),
+            pltpu.VMEM((1024, 256), F32),
+            pltpu.SemaphoreType.DMA((4,)),
         ],
         compiler_params=params(16),
         cost_estimate=cost(2_000_000_000, 3_000_000),
@@ -658,22 +725,25 @@
     student_w2,
 ):
     tw1, tw2, sw1, sw2 = map(taps_first, (teacher_w1, teacher_w2, student_w1, student_w2))
-    main, to_pair, to_cross = relay(brick_feats.reshape(1024, 256))
-    edge_cross = swap_cross(to_cross)
-    edge_pair = swap_pair(to_pair)
     feats = window_feats.reshape(window_feats.shape[0], 2048, 128)
     tables = (window_brick, window_z, window_count)
-    sum_pair, sum_cross, *kept = teacher_outer(*tables, feats, gaussian, tw1, tw2, to_pair)
+    sum_pair, sum_cross, *kept = teacher_outer(*tables, feats, gaussian, tw1, tw2)
+    big1, big2, held_feats, held_gauss = kept
+    got_pair = swap_pair(sum_pair)
     got_cross = swap_cross(sum_cross)
-    got_pair = swap_pair(sum_pair)
-    big1, big2, held_feats, held_gauss = kept
-    own = teacher_own(*tables, held_feats, held_gauss, big1, big2, edge_pair, edge_cross)
-    prob, slope = forward(main, edge_pair, edge_cross, sw1, sw2)
-    teacher_sum, grad, grad_pair, grad_cross = combine(own, got_pair, got_cross, prob)
+    main, to_pair, to_cross = relay(brick_feats.reshape(1024, 256), held_gauss)
+    edge_pair = swap_pair(to_pair)
+    edge_cross = swap_cross(to_cross)
+    own = teacher_own(*tables, held_feats, held_gauss, big1, big2)
+    prob, slope, hidden, *bigs = forward(main, sw1, sw2)
+    sums = (own, got_pair, got_cross)
+    grad_pair, grad_cross, grad, slope_ends = edge_grads(
+        main, edge_pair, edge_cross, hidden, *bigs, *sums
+    )
+    near_pair = swap_pair(grad_pair)
     near_cross = swap_cross(grad_cross)
-    near_pair = swap_pair(grad_pair)
-    early = inner(grad, slope, sw1, sw2)
-    feature_grad = outer_rows(grad, near_pair, near_cross, slope, *early)
+    teacher_sum, *early = inner(*sums, prob, grad, slope, sw1, sw2)
+    feature_grad = outer_rows(grad, near_pair, near_cross, slope_ends, *early)
     return (teacher_sum.reshape(16, 4, 8, 256), feature_grad.reshape(32, 4, 8, 256))
 
 

time: 40.4 us -> 38.4 us (0.950); the launches traced: 39.6 us -> 38.2 us
  waiting for transfers between devices: 3.97 us -> 2.35 us
    ppermute x3, waiting for transfers between devices: 3.97 us -> 2.34 us  [swap_cross(): return lax.ppermute(value, 'gy', pairs + [(j, i) for i, j in pairs])]
  transfers between devices with their start and end apart: 6 -> 6, of which waited for: 1 -> 1; matrix products, arithmetic and copies ran while one was open for 0% -> 0% of each run, Pallas kernels for 42% -> 29%
where the time goes in v2:
time: 38.4 us; the launch traced here: 38.2 us
  Pallas kernels  22.1 us (58%)
  starting transfers between devices  12.8 us (33%)
  waiting for transfers between devices  2.35 us (6%)
  between operations  0.92 us (2%)
    ppermute x3, starting transfers between devices, swap_cross(): return lax.ppermute(value, 'gy', pairs + [(j, i) for i, j in pairs])  12.5 us
    pallas_call x1, Pallas kernels, teacher_outer(): pl.pallas_call(outer_kernel, name='teacher_outer', grid_spec=pltpu.Prefet...  7.23 us
    pallas_call x1, Pallas kernels, teacher_own(): pl.pallas_call(own_kernel, name='teacher_own', grid_spec=pltpu.PrefetchSc...  5.2 us
    pallas_call x1, Pallas kernels, inner(): pl.pallas_call(inner_kernel, name='inner', in_specs=[VMEM] * 8, out_specs...  2.64 us
    pallas_call x1, Pallas kernels, outer_rows(): pl.pallas_call(outer_rows_kernel, name='outer_rows', in_specs=[VMEM] * 9,...  2.54 us
    ppermute x3, waiting for transfers between devices, swap_cross(): return lax.ppermute(value, 'gy', pairs + [(j, i) for i, j in pairs])  2.34 us
    pallas_call x1, Pallas kernels, forward(): pl.pallas_call(forward_kernel, name='forward', in_specs=[VMEM] * 3, out_s...  1.9 us
    pallas_call x1, Pallas kernels, edge_grads(): pl.pallas_call(edge_kernel, name='edge_grads', in_specs=[VMEM] * 9, out_s...  1.38 us
  transfers between devices with their start and end apart: 6, of which 1 were waited for; matrix products, arithmetic and copies ran while one was open for 0% of the time, Pallas kernels for 29%

profile of v2, /device:TPU:1, one launch (start us, length us, event | category | flops | bytes accessed | tf_op | source)
XLA Modules:
  0.0 38.2 jit_solution(3873370685940324901)
XLA Ops:
  0.6 7.2 %teacher_outer.1 = (f32[8,64,256]{2,1,0:T(8,128)S(1)}, f32[8,64,256]{2,1,0:T(8,128)S(1)}, bf16[256,1536]{1,0:T(8,128)(2,1)S(1)}, bf16[128,1536]{1,0:T(8,128)(2,1...) custom-call(s32[64]{0:T(128)} %brick_s.3, s32[64]{0:T(128)} %z_s.3, s32[16]{0:T(128)} %count_s.3, ...), custom_call_target="tpu_custom_call" | custom-call | flops 5000000000 | bytes 4000000 | tf_op jit(solution)/shard_map/teacher_outer/pallas_call | solution.py:324
  7.9 0.1 collective-permute-start
  8.0 4.5 %collective-permute-start.1 = (f32[8,64,256]{2,1,0:T(8,128)S(1)}, f32[8,64,256]{2,1,0:T(8,128)S(1)}, u32[]{:S(2)}, u32[]{:S(2)}) collective-permute-start(f32[8,64,256]{2,1,0:T(8,128)S(1)} %get-tuple-element.31), channel_id=1, source_target_pairs={{1,2},{3,4},{5,6},{7,8},{9,10},{11,12},{13,14},{2,1},{4,3},{6,5},{... | collective-permute-start | bytes 1572872 | tf_op jit(solution)/shard_map/ppermute | solution.py:707
  12.5 1.2 %relay.1 = (bf16[8,128,256]{2,1,0:T(8,128)(2,1)S(1)}, bf16[2,128,256]{2,1,0:T(8,128)(2,1)S(1)}, bf16[2,128,256]{2,1,0:T(8,128)(2,1)S(1)}) custom-call(bf16[1024,256]{1,0:T(8,128)(2,1)} %bitcast.20, f32[4,16,128]{2,1,0:T(8,128)S(1)} %get-tuple-element.27.gauss_ref.behind), custom_call_target="tpu_custom_call" | custom-call | bytes 1500000 | tf_op jit(solution)/shard_map/relay/pallas_call | solution.py:388
  13.7 0.1 collective-permute-start.2
  13.8 3.7 %collective-permute-start.3 = (bf16[2,128,256]{2,1,0:T(8,128)(2,1)S(1)}, bf16[2,128,256]{2,1,0:T(8,128)(2,1)S(1)}, u32[]{:S(2)}, u32[]{:S(2)}) collective-permute-start(bf16[2,128,256]{2,1,0:T(8,128)(2,1)S(1)} %get-tuple-element.35), channel_id=1, source_target_pairs={{1,2},{3,4},{5,6},{7,8},{9,10},{11,12},{13,14},{2,1},{4,3},{6,5},{... | collective-permute-start | bytes 393224 | tf_op jit(solution)/shard_map/ppermute | solution.py:707
  17.5 0.0 copy-start
  17.5 0.0 copy-start.1
  17.5 5.2 %teacher_own.1.own_ref = f32[8,64,256]{2,1,0:T(8,128)S(1)} custom-call(s32[64]{0:T(128)} %brick_s.3, s32[64]{0:T(128)} %z_s.3, s32[16]{0:T(128)} %count_s.3, bf16[4,2048,128]{2,1,0:T(8,128)(2,1)S(1)} %get-tuple-element.26.feats_ref, f32[4,16,128]{2,1,0:T(8,128)S(1)} %get-tuple-element.27.gauss_ref.behind, bf16[256,1536]{1,0:T(8,128)(2,1)S(1)} %get-tuple-element.28.big1, ...), custom_call_target="tpu_custom_call" | custom-call | flops 4000000000 | bytes 3000000 | tf_op jit(solution)/shard_map/teacher_own/pallas_call | solution.py:349
  22.7 0.0 copy-done
  22.7 0.0 copy-done.1
  22.7 1.9 %forward.1 = (f32[4,64,256]{2,1,0:T(8,128)S(1)}, f32[6,128,256]{2,1,0:T(8,128)S(1)}, bf16[3,6,128,256]{3,2,1,0:T(8,128)(2,1)S(1)}, bf16[256,1536]{1,0:T(8,128)(2,1)S(1)}, bf16[128,1536]{1,0:T(8,128)(2,1)S(1)}) custom-call(bf16[8,128,256]{2,1,0:T(8,128)(2,1)S(1)} %get-tuple-element.32.main_ref, bf16[3,9,32,32]{3,2,1,0:T(8,128)(2,1)S(1)} %bitcast.16, ...), custom_call_target="tpu_custom_call" | custom-call | flops 4000000000 | bytes 3000000 | tf_op jit(solution)/shard_map/forward/pallas_call | solution.py:459
  24.6 0.0 collective-permute-done.2.pair_in
  24.7 2.3 %collective-permute-done.3.cross_in = bf16[2,128,256]{2,1,0:T(8,128)(2,1)S(1)} collective-permute-done((bf16[2,128,256]{2,1,0:T(8,128)(2,1)S(1)}, bf16[2,128,256]{2,1,0:T(8,128)(2,1)S(1)}, u32[]{:S(2)}, u32[]{:S(2)}) %collective-permute-start.3) | collective-permute-done | bytes 131104 | tf_op jit(solution)/shard_map/ppermute | solution.py:707
  27.0 0.0 collective-permute-done.from_pair_ref
  27.0 0.0 collective-permute-done.1.from_cross_ref
  27.0 1.4 %edge_grads.1 = (bf16[2,64,256]{2,1,0:T(8,128)(2,1)S(1)}, bf16[2,64,256]{2,1,0:T(8,128)(2,1)S(1)}, bf16[4,64,256]{2,1,0:T(8,128)(2,1)S(1)}, f32[4,128,256]{2,1,0:T(8,128)S(1)}) custom-call(bf16[8,128,256]{2,1,0:T(8,128)(2,1)S(1)} %get-tuple-element.32.main_ref, bf16[2,128,256]{2,1,0:T(8,128)(2,1)S(1)} %collective-permute-done.2.pair_in, ...), custom_call_target="tpu_custom_call" | custom-call | flops 2000000000 | bytes 3000000 | tf_op jit(solution)/shard_map/edge_grads/pallas_call | solution.py:522
  28.4 0.1 collective-permute-start.4
  28.5 4.4 %collective-permute-start.5 = (bf16[2,64,256]{2,1,0:T(8,128)(2,1)S(1)}, bf16[2,64,256]{2,1,0:T(8,128)(2,1)S(1)}, u32[]{:S(2)}, u32[]{:S(2)}) collective-permute-start(bf16[2,64,256]{2,1,0:T(8,128)(2,1)S(1)} %get-tuple-element.43), channel_id=1, source_target_pairs={{1,2},{3,4},{5,6},{7,8},{9,10},{11,12},{13,14},{2,1},{4,3},{6,5},{... | collective-permute-start | bytes 196616 | tf_op jit(solution)/shard_map/ppermute | solution.py:707
  32.9 2.6 %inner.1 = (f32[512,256]{1,0:T(8,128)}, f32[1024,128]{1,0:T(8,128)S(1)}, f32[1024,128]{1,0:T(8,128)S(1)}, bf16[3,6,128,256]{3,2,1,0:T(8,128)(2,1)S(1)}, bf16[256...) custom-call(f32[8,64,256]{2,1,0:T(8,128)S(1)} %teacher_own.1.own_ref, ...), custom_call_target="tpu_custom_call" | custom-call | flops 4000000000 | bytes 3000000 | tf_op jit(solution)/shard_map/inner/pallas_call | solution.py:605
  35.5 0.0 collective-permute-done.4.pair_ref
  35.5 0.0 collective-permute-done.5.cross_ref
  35.5 2.5 %outer_rows.1 = f32[1024,256]{1,0:T(8,128)} custom-call(bf16[4,64,256]{2,1,0:T(8,128)(2,1)S(1)} %get-tuple-element.39.grad_ref.main_ref, bf16[2,64,256]{2,1,0:T(8,128)(2,1)S(1)} %collective-permute-done.4.pair_ref, bf16[2,64,256]{2,1,0:T(8,128)(2,1)S(1)} %collective-permute-done.5.cross_ref, f32[4,128,256]{2,1,0:T(8,128)S(1)} %get-tuple-element.44.slope_ref, ...), custom_call_target="tpu_custom_call" | custom-call | flops 2000000000 | bytes 3000000 | tf_op jit(solution)/shard_map/outer_rows/pallas_call | solution.py:680
Async XLA Ops:
  7.9 19.1 %collective-permute-start = (f32[8,64,256]{2,1,0:T(8,128)S(1)}, f32[8,64,256]{2,1,0:T(8,128)S(1)}, u32[]{:S(2)}, u32[]{:S(2)}) collective-permute-start(f32[8,64,256]{2,1,0:T(8,128)S(1)} %get-tuple-element.30), channel_id=1, source_target_pairs={{0,1},{1,0},{2,3},{3,2},{4,5},{5,4},{6,7},{7,6},{8,9},{9,8},{10,11... | collective-permute-start | bytes 1572872 | tf_op jit(solution)/shard_map/ppermute | solution.py:701
  8.0 19.0 %collective-permute-start.1 = (f32[8,64,256]{2,1,0:T(8,128)S(1)}, f32[8,64,256]{2,1,0:T(8,128)S(1)}, u32[]{:S(2)}, u32[]{:S(2)}) collective-permute-start(f32[8,64,256]{2,1,0:T(8,128)S(1)} %get-tuple-element.31), channel_id=1, source_target_pairs={{1,2},{3,4},{5,6},{7,8},{9,10},{11,12},{13,14},{2,1},{4,3},{6,5},{... | collective-permute-start | bytes 1572872 | tf_op jit(solution)/shard_map/ppermute | solution.py:707
  13.7 10.9 %collective-permute-start.2 = (bf16[2,128,256]{2,1,0:T(8,128)(2,1)S(1)}, bf16[2,128,256]{2,1,0:T(8,128)(2,1)S(1)}, u32[]{:S(2)}, u32[]{:S(2)}) collective-permute-start(bf16[2,128,256]{2,1,0:T(8,128)(2,1)S(1)} %get-tuple-element.34), channel_id=1, source_target_pairs={{0,1},{1,0},{2,3},{3,2},{4,5},{5,4},{6,7},{7,6},{8,9},{9,8},{10,11... | collective-permute-start | bytes 393224 | tf_op jit(solution)/shard_map/ppermute | solution.py:701
  13.8 13.2 %collective-permute-start.3 = (bf16[2,128,256]{2,1,0:T(8,128)(2,1)S(1)}, bf16[2,128,256]{2,1,0:T(8,128)(2,1)S(1)}, u32[]{:S(2)}, u32[]{:S(2)}) collective-permute-start(bf16[2,128,256]{2,1,0:T(8,128)(2,1)S(1)} %get-tuple-element.35), channel_id=1, source_target_pairs={{1,2},{3,4},{5,6},{7,8},{9,10},{11,12},{13,14},{2,1},{4,3},{6,5},{... | collective-permute-start | bytes 393224 | tf_op jit(solution)/shard_map/ppermute | solution.py:707
  17.5 5.2 %copy-start = (bf16[32,32,3,3,3]{1,0,4,3,2:T(8,128)(2,1)S(1)}, bf16[32,32,3,3,3]{1,0,4,3,2:T(8,128)(2,1)}, u32[]{:S(2)}) copy-start(bf16[32,32,3,3,3]{1,0,4,3,2:T(8,128)(2,1)} %param.18) | copy-start | bytes 165892
  17.5 5.2 %copy-start.1 = (bf16[16,32,3,3,3]{1,0,4,3,2:T(8,128)(2,1)S(1)}, bf16[16,32,3,3,3]{1,0,4,3,2:T(8,128)(2,1)}, u32[]{:S(2)}) copy-start(bf16[16,32,3,3,3]{1,0,4,3,2:T(8,128)(2,1)} %param.19) | copy-start | bytes 82948
  28.4 7.1 %collective-permute-start.4 = (bf16[2,64,256]{2,1,0:T(8,128)(2,1)S(1)}, bf16[2,64,256]{2,1,0:T(8,128)(2,1)S(1)}, u32[]{:S(2)}, u32[]{:S(2)}) collective-permute-start(bf16[2,64,256]{2,1,0:T(8,128)(2,1)S(1)} %get-tuple-element.42), channel_id=1, source_target_pairs={{0,1},{1,0},{2,3},{3,2},{4,5},{5,4},{6,7},{7,6},{8,9},{9,8},{10,11... | collective-permute-start | bytes 196616 | tf_op jit(solution)/shard_map/ppermute | solution.py:701
  28.5 7.1 %collective-permute-start.5 = (bf16[2,64,256]{2,1,0:T(8,128)(2,1)S(1)}, bf16[2,64,256]{2,1,0:T(8,128)(2,1)S(1)}, u32[]{:S(2)}, u32[]{:S(2)}) collective-permute-start(bf16[2,64,256]{2,1,0:T(8,128)(2,1)S(1)} %get-tuple-element.43), channel_id=1, source_target_pairs={{1,2},{3,4},{5,6},{7,8},{9,10},{11,12},{13,14},{2,1},{4,3},{6,5},{... | collective-permute-start | bytes 196616 | tf_op jit(solution)/shard_map/ppermute | solution.py:707

commit v3 on v2

--- a/solution.py
+++ b/solution.py
@@ -218,8 +218,8 @@
     gauss_hbm,
     w1_hbm,
     w2_hbm,
-    pair_ref,
     cross_ref,
+    total,
     big1,
     big2,
     feats_ref,
@@ -229,7 +229,6 @@
     flat,
     xbuf,
     hbuf,
-    total,
     sems,
 ):
     slots = feats_ref.shape[0]
@@ -269,9 +268,7 @@
         xbuf,
         hbuf,
     )
-    odd = parity()
-    pair_ref[...] = total[1 - odd]
-    cross_ref[...] = total[odd]
+    cross_ref[...] = total[parity()]
 
 
 def own_kernel(
@@ -282,12 +279,19 @@
     gauss_ref,
     big1,
     big2,
+    total,
+    main_ref,
     own_ref,
+    pair_ref,
+    edge_ref,
     flat,
     xbuf,
     hbuf,
 ):
     own_ref[...] = jnp.zeros_like(own_ref)
+    odd = parity()
+    pair_ref[...] = total[1 - odd]
+    edge_ref[...] = main_ref[pl.ds(6 * (1 - odd), 2)]
 
     def store(mine, row, low, high):
         own_ref[row, :, pl.ds(0, 128)] += low
@@ -309,6 +313,7 @@
 
 
 SUMS = jax.ShapeDtypeStruct((8, 64, 256), F32)
+EDGE = jax.ShapeDtypeStruct((2, 128, 256), BF16)
 
 
 def teacher_scratch(slots):
@@ -330,11 +335,11 @@
             out_specs=[VMEM] * 6,
             scratch_shapes=[pltpu.VMEM(w1.shape, BF16), pltpu.VMEM(w2.shape, BF16)]
             + teacher_scratch(slots)
-            + [pltpu.VMEM((2, 8, 64, 256), F32), pltpu.SemaphoreType.DMA((slots + 3,))],
+            + [pltpu.SemaphoreType.DMA((slots + 3,))],
         ),
         out_shape=[
             SUMS,
-            SUMS,
+            jax.ShapeDtypeStruct((2, 8, 64, 256), F32),
             jax.ShapeDtypeStruct((256, 1536), BF16),
             jax.ShapeDtypeStruct((128, 1536), BF16),
             jax.ShapeDtypeStruct(feats.shape, BF16),
@@ -345,24 +350,23 @@
     )(*map(in_hbm, (brick, z, count, feats, gauss, w1, w2)))
 
 
-def teacher_own(brick, z, count, feats, gauss, big1, big2):
+def teacher_own(brick, z, count, feats, gauss, big1, big2, total, main):
     return pl.pallas_call(
         own_kernel,
         name="teacher_own",
         grid_spec=pltpu.PrefetchScalarGridSpec(
             num_scalar_prefetch=3,
-            in_specs=[VMEM] * 4,
-            out_specs=VMEM,
+            in_specs=[VMEM] * 6,
+            out_specs=[VMEM] * 3,
             scratch_shapes=teacher_scratch(feats.shape[0]),
         ),
-        out_shape=SUMS,
+        out_shape=[SUMS, SUMS, EDGE],
         compiler_params=params(28),
         cost_estimate=cost(4_000_000_000, 3_000_000),
-    )(*map(in_hbm, (brick, z, count)), feats, gauss, big1, big2)
-
-
-def relay_kernel(feats_hbm, behind, main_ref, pair_ref, cross_ref, feats_ref, flat, sems):
-    odd = parity()
+    )(*map(in_hbm, (brick, z, count)), feats, gauss, big1, big2, total, main)
+
+
+def relay_kernel(feats_hbm, behind, main_ref, cross_ref, feats_ref, flat, sems):
     chunks = 4
     rows = 1024 // chunks
     loads = []
@@ -379,18 +383,16 @@
                 main_ref[y, pl.ds(i * rows // 8, rows // 8), pl.ds(h * 128, 128)] = flat[
                     h, pl.ds(i * rows + y, rows // 8, stride=8), :
                 ].astype(BF16)
-    pair_ref[...] = main_ref[pl.ds(6 * (1 - odd), 2)]
-    cross_ref[...] = main_ref[pl.ds(6 * odd, 2)]
+    cross_ref[...] = main_ref[pl.ds(6 * parity(), 2)]
 
 
 def relay(feats, behind):
-    edge = jax.ShapeDtypeStruct((2, 128, 256), BF16)
     return pl.pallas_call(
         relay_kernel,
         name="relay",
         in_specs=[HBM, VMEM],
-        out_specs=[VMEM] * 3,
-        out_shape=[jax.ShapeDtypeStruct((8, 128, 256), BF16), edge, edge],
+        out_specs=[VMEM] * 2,
+        out_shape=[jax.ShapeDtypeStruct((8, 128, 256), BF16), EDGE],
         scratch_shapes=[
             pltpu.VMEM((1024, 256), BF16),
             pltpu.VMEM((2, 1024, 128), F32),
@@ -434,7 +436,9 @@
     return pre * sig, sig * (1.0 + pre * (1.0 - sig))
 
 
-def forward_kernel(main_ref, w1_ref, w2_ref, prob_ref, slope_ref, hbuf, big1, big2, xbuf):
+def forward_kernel(
+    main_ref, w1_ref, w2_ref, prob_ref, slope_ref, hbuf, big1, big2, back1, back2, xbuf
+):
     fill_big(big1, band(w1_ref, False), 2)
     fill_big(big2, band(w2_ref, True), 2)
     for y in range(4):
@@ -453,6 +457,10 @@
         logits = jnp.dot(big2[...], window(hbuf, y, 4), preferred_element_type=F32)
         for k in range(2):
             prob_ref[y + k] = class_softmax(logits[k * 64 : (k + 1) * 64])
+    flip2 = band(w2_ref, True)
+    fill_big(back2, [flip2[8 - t].T for t in range(9)], 2)
+    flip1 = band(w1_ref, True)
+    fill_big(back1, [flip1[8 - t].T for t in range(9)], 2)
 
 
 def forward(main, w1, w2):
@@ -460,13 +468,15 @@
         forward_kernel,
         name="forward",
         in_specs=[VMEM] * 3,
-        out_specs=[VMEM] * 5,
+        out_specs=[VMEM] * 7,
         out_shape=[
             jax.ShapeDtypeStruct((4, 64, 256), F32),
             jax.ShapeDtypeStruct((6, 128, 256), F32),
             jax.ShapeDtypeStruct((3, 6, 128, 256), BF16),
             jax.ShapeDtypeStruct((256, 1536), BF16),
             jax.ShapeDtypeStruct((128, 1536), BF16),
+            jax.ShapeDtypeStruct((256, 1536), BF16),
+            jax.ShapeDtypeStruct((256, 768), BF16),
         ],
         scratch_shapes=[pltpu.VMEM((3, 8, 128, 256), BF16)],
         compiler_params=params(16),
@@ -476,8 +486,8 @@
 
 def edge_kernel(
     main_ref,
+    cross_in,
     pair_in,
-    cross_in,
     hin_ref,
     big1,
     big2,
@@ -517,7 +527,7 @@
     cross_ref[...] = grad_ref[pl.ds(2 * odd, 2)]
 
 
-def edge_grads(main, pair, cross, hidden, big1, big2, own, from_pair, from_cross):
+def edge_grads(main, cross, pair, hidden, big1, big2, own, from_pair, from_cross):
     edge = jax.ShapeDtypeStruct((2, 64, 256), BF16)
     return pl.pallas_call(
         edge_kernel,
@@ -536,7 +546,7 @@
         ],
         compiler_params=params(12),
         cost_estimate=cost(2_000_000_000, 3_000_000),
-    )(main, pair, cross, hidden, big1, big2, own, from_pair, from_cross)
+    )(main, cross, pair, hidden, big1, big2, own, from_pair, from_cross)
 
 
 def put_out(turns, y, grad):
@@ -556,14 +566,12 @@
     prob_ref,
     grad_ref,
     slope_ref,
-    w1_ref,
-    w2_ref,
+    big1,
+    big2,
     sum_hbm,
     turn0,
     turn1,
     pbuf,
-    big1,
-    big2,
     gbuf,
     sum0,
     sum1,
@@ -586,10 +594,6 @@
     sum_ref[:, pl.ds(128, 128)] = sum1[...]
     copy = pltpu.make_async_copy(sum_ref, sum_hbm, sem)
     copy.start()
-    flip2 = band(w2_ref, True)
-    fill_big(big2, [flip2[8 - t].T for t in range(9)], 2)
-    flip1 = band(w1_ref, True)
-    fill_big(big1, [flip1[8 - t].T for t in range(9)], 2)
     for y in range(0, 6, 2):
         grad = jnp.dot(big2[...], window(gbuf, y, 4), preferred_element_type=F32)
         for k in range(2):
@@ -600,20 +604,18 @@
     copy.wait()
 
 
-def inner(own, from_pair, from_cross, prob, grad, slope, w1, w2):
+def inner(own, from_pair, from_cross, prob, grad, slope, big1, big2):
     turned = jax.ShapeDtypeStruct((1024, 128), F32)
     return pl.pallas_call(
         inner_kernel,
         name="inner",
         in_specs=[VMEM] * 8,
-        out_specs=[HBM] + [VMEM] * 5,
+        out_specs=[HBM] + [VMEM] * 3,
         out_shape=[
             jax.ShapeDtypeStruct((512, 256), F32),
             turned,
             turned,
             jax.ShapeDtypeStruct((3, 6, 128, 256), BF16),
-            jax.ShapeDtypeStruct((256, 1536), BF16),
-            jax.ShapeDtypeStruct((256, 768), BF16),
         ],
         scratch_shapes=[
             pltpu.VMEM((3, 8, 64, 256), BF16),
@@ -624,13 +626,13 @@
         ],
         compiler_params=params(16),
         cost_estimate=cost(4_000_000_000, 3_000_000),
-    )(own, from_pair, from_cross, prob, grad, slope, w1, w2)
+    )(own, from_pair, from_cross, prob, grad, slope, big1, big2)
 
 
 def outer_rows_kernel(
     main_ref,
+    cross_ref,
     pair_ref,
-    cross_ref,
     slope_ref,
     done0,
     done1,
@@ -658,42 +660,49 @@
             v = grad[k * 128 : (k + 1) * 128] * slope_ref[g // 2 + k]
             keep = inside(row + k)
             put_row(pbuf, p + k, v if keep is None else v * keep)
-    for p, row in ((0, 0), (4, 6)):
-        grad = jnp.dot(big1[...], window(pbuf, p, 4), preferred_element_type=F32)
-        put_out((turn0, turn1), row, grad)
-    chunks = 4
-    rows = 1024 // chunks
-    y = lax.broadcasted_iota(jnp.int32, (rows, 128), 0) % 8
+    y = lax.broadcasted_iota(jnp.int32, (32, 16, 128), 1) % 8
     early = (y >= 2) & (y < 6)
     copies = []
-    for i in range(chunks):
-        part = pl.ds(i * rows, rows)
-        out_ref[part, pl.ds(0, 128)] = jnp.where(early, done0[part], turn0[part])
-        out_ref[part, pl.ds(128, 128)] = jnp.where(early, done1[part], turn1[part])
-        copies.append(pltpu.make_async_copy(out_ref.at[part], out_hbm.at[part], sems.at[i]))
+    for i in range(2):
+        half = jnp.concatenate([big1[pl.ds(k * 128 + i * 64, 64)] for k in range(2)], axis=0)
+        for p, row in ((0, 0), (4, 6)):
+            grad = jnp.dot(half, window(pbuf, p, 4), preferred_element_type=F32)
+            for k in range(2):
+                for x in range(2):
+                    for h, turn in enumerate((turn0, turn1)):
+                        at = k * 64 + x * 32
+                        turn[pl.ds((2 * i + x) * 8 + row + k, 32, stride=32), :] = grad[
+                            at : at + 32, h * 128 : (h + 1) * 128
+                        ]
+        part = pl.ds(i * 16, 16)
+        for h, (turn, done) in enumerate(((turn0, done0), (turn1, done1))):
+            late = turn.reshape(32, 32, 128)[:, part]
+            kept = done.reshape(32, 32, 128)[:, part]
+            out_ref[i, :, :, pl.ds(h * 128, 128)] = jnp.where(early, kept, late)
+        copies.append(pltpu.make_async_copy(out_ref.at[i], out_hbm.at[:, part], sems.at[i]))
         copies[i].start()
     for copy in copies:
         copy.wait()
 
 
-def outer_rows(main, pair, cross, slope, done0, done1, pin, big1, big2):
+def outer_rows(main, cross, pair, slope, done0, done1, pin, big1, big2):
     return pl.pallas_call(
         outer_rows_kernel,
         name="outer_rows",
         in_specs=[VMEM] * 9,
         out_specs=HBM,
-        out_shape=jax.ShapeDtypeStruct((1024, 256), F32),
+        out_shape=jax.ShapeDtypeStruct((32, 32, 256), F32),
         scratch_shapes=[
             pltpu.VMEM((3, 8, 64, 256), BF16),
             pltpu.VMEM((3, 8, 128, 256), BF16),
             pltpu.VMEM((1024, 128), F32),
             pltpu.VMEM((1024, 128), F32),
-            pltpu.VMEM((1024, 256), F32),
-            pltpu.SemaphoreType.DMA((4,)),
+            pltpu.VMEM((2, 32, 16, 256), F32),
+            pltpu.SemaphoreType.DMA((2,)),
         ],
         compiler_params=params(16),
         cost_estimate=cost(2_000_000_000, 3_000_000),
-    )(main, pair, cross, slope, done0, done1, pin, big1, big2)
+    )(main, cross, pair, slope, done0, done1, pin, big1, big2)
 
 
 def swap_pair(value):
@@ -727,23 +736,26 @@
     tw1, tw2, sw1, sw2 = map(taps_first, (teacher_w1, teacher_w2, student_w1, student_w2))
     feats = window_feats.reshape(window_feats.shape[0], 2048, 128)
     tables = (window_brick, window_z, window_count)
-    sum_pair, sum_cross, *kept = teacher_outer(*tables, feats, gaussian, tw1, tw2)
-    big1, big2, held_feats, held_gauss = kept
+    sum_cross, sides, big1, big2, held_feats, held_gauss = teacher_outer(
+        *tables, feats, gaussian, tw1, tw2
+    )
+    got_cross = swap_cross(sum_cross)
+    main, to_cross = relay(brick_feats.reshape(1024, 256), held_gauss)
+    edge_cross = swap_cross(to_cross)
+    own, sum_pair, to_pair = teacher_own(
+        *tables, held_feats, held_gauss, big1, big2, sides, main
+    )
     got_pair = swap_pair(sum_pair)
-    got_cross = swap_cross(sum_cross)
-    main, to_pair, to_cross = relay(brick_feats.reshape(1024, 256), held_gauss)
     edge_pair = swap_pair(to_pair)
-    edge_cross = swap_cross(to_cross)
-    own = teacher_own(*tables, held_feats, held_gauss, big1, big2)
-    prob, slope, hidden, *bigs = forward(main, sw1, sw2)
+    prob, slope, hidden, near1, near2, back1, back2 = forward(main, sw1, sw2)
     sums = (own, got_pair, got_cross)
     grad_pair, grad_cross, grad, slope_ends = edge_grads(
-        main, edge_pair, edge_cross, hidden, *bigs, *sums
+        main, edge_cross, edge_pair, hidden, near1, near2, *sums
     )
     near_pair = swap_pair(grad_pair)
     near_cross = swap_cross(grad_cross)
-    teacher_sum, *early = inner(*sums, prob, grad, slope, sw1, sw2)
-    feature_grad = outer_rows(grad, near_pair, near_cross, slope_ends, *early)
+    teacher_sum, *early = inner(*sums, prob, grad, slope, back1, back2)
+    feature_grad = outer_rows(grad, near_cross, near_pair, slope_ends, *early, back1, back2)
     return (teacher_sum.reshape(16, 4, 8, 256), feature_grad.reshape(32, 4, 8, 256))
 
 

time: 38.4 us -> 37.9 us (0.987); the launches traced: 38.2 us -> 37.3 us
  waiting for transfers between devices: 2.35 us -> 1.74 us
    ppermute x3, waiting for transfers between devices: 2.34 us -> 1.73 us  [swap_cross(): return lax.ppermute(value, 'gy', pairs + [(j, i) for i, j in pairs])]
    pallas_call x1, Pallas kernels: 2.64 us -> 2.06 us  [inner(): pl.pallas_call(inner_kernel, name='inner', in_specs=[VMEM] * 8, out_specs...]
    pallas_call x1, Pallas kernels: 1.9 us -> 2.41 us  [forward(): pl.pallas_call(forward_kernel, name='forward', in_specs=[VMEM] * 3, out_s...]
where the time goes in v3:
time: 37.9 us; the launch traced here: 37.3 us
  Pallas kernels  21.8 us (58%)
  starting transfers between devices  12.8 us (34%)
  waiting for transfers between devices  1.74 us (5%)
  between operations  0.92 us (2%)
    ppermute x3, starting transfers between devices, swap_cross(): return lax.ppermute(value, 'gy', pairs + [(j, i) for i, j in pairs])  12.2 us
    pallas_call x1, Pallas kernels, teacher_outer(): pl.pallas_call(outer_kernel, name='teacher_outer', grid_spec=pltpu.Prefet...  7.1 us
    pallas_call x1, Pallas kernels, teacher_own(): pl.pallas_call(own_kernel, name='teacher_own', grid_spec=pltpu.PrefetchSc...  5.25 us
    pallas_call x1, Pallas kernels, forward(): pl.pallas_call(forward_kernel, name='forward', in_specs=[VMEM] * 3, out_s...  2.41 us
    pallas_call x1, Pallas kernels, outer_rows(): pl.pallas_call(outer_rows_kernel, name='outer_rows', in_specs=[VMEM] * 9,...  2.36 us
    pallas_call x1, Pallas kernels, inner(): pl.pallas_call(inner_kernel, name='inner', in_specs=[VMEM] * 8, out_specs...  2.06 us
    ppermute x3, waiting for transfers between devices, swap_cross(): return lax.ppermute(value, 'gy', pairs + [(j, i) for i, j in pairs])  1.73 us
    pallas_call x1, Pallas kernels, edge_grads(): pl.pallas_call(edge_kernel, name='edge_grads', in_specs=[VMEM] * 9, out_s...  1.37 us
  transfers between devices with their start and end apart: 6, of which 1 were waited for; matrix products, arithmetic and copies ran while one was open for 0% of the time, Pallas kernels for 29%

profile of v3, /device:TPU:1, one launch (start us, length us, event | category | flops | bytes accessed | tf_op | source)
XLA Modules:
  0.0 37.3 jit_solution(15447184944988040735)
XLA Ops:
  0.6 7.1 %teacher_outer.1 = (f32[8,64,256]{2,1,0:T(8,128)S(1)}, f32[2,8,64,256]{3,2,1,0:T(8,128)S(1)}, bf16[256,1536]{1,0:T(8,128)(2,1)S(1)}, bf16[128,1536]{1,0:T(8,128)...) custom-call(s32[64]{0:T(128)} %brick_s.3, s32[64]{0:T(128)} %z_s.3, s32[16]{0:T(128)} %count_s.3, ...), custom_call_target="tpu_custom_call" | custom-call | flops 5000000000 | bytes 4000000 | tf_op jit(solution)/shard_map/teacher_outer/pallas_call | solution.py:329
  7.7 4.5 %collective-permute-start.1 = (f32[8,64,256]{2,1,0:T(8,128)S(1)}, f32[8,64,256]{2,1,0:T(8,128)S(1)}, u32[]{:S(2)}, u32[]{:S(2)}) collective-permute-start(f32[8,64,256]{2,1,0:T(8,128)S(1)} %get-tuple-element.36), channel_id=1, source_target_pairs={{1,2},{3,4},{5,6},{7,8},{9,10},{11,12},{13,14},{2,1},{4,3},{6,5},{... | collective-permute-start | bytes 1572872 | tf_op jit(solution)/shard_map/ppermute | solution.py:716
  12.3 1.2 %relay.1 = (bf16[8,128,256]{2,1,0:T(8,128)(2,1)S(1)}, bf16[2,128,256]{2,1,0:T(8,128)(2,1)S(1)}) custom-call(bf16[1024,256]{1,0:T(8,128)(2,1)} %bitcast.18, f32[4,16,128]{2,1,0:T(8,128)S(1)} %get-tuple-element.29.behind.gauss_ref), custom_call_target="tpu_custom_call" | custom-call | bytes 1500000 | tf_op jit(solution)/shard_map/relay/pallas_call | solution.py:390
  13.5 0.0 copy-start
  13.5 0.0 copy-start.1
  13.6 5.3 %teacher_own.1 = (f32[8,64,256]{2,1,0:T(8,128)S(1)}, f32[8,64,256]{2,1,0:T(8,128)S(1)}, bf16[2,128,256]{2,1,0:T(8,128)(2,1)S(1)}) custom-call(s32[64]{0:T(128)} %brick_s.3, s32[64]{0:T(128)} %z_s.3, s32[16]{0:T(128)} %count_s.3, bf16[4,2048,128]{2,1,0:T(8,128)(2,1)S(1)} %get-tuple-element.28.feats_ref, f32[4,16,128]{2,1,0:T(8,128)S(1)} %get-tuple-element.29.behind.gauss_ref, ...), custom_call_target="tpu_custom_call" | custom-call | flops 4000000000 | bytes 3000000 | tf_op jit(solution)/shard_map/teacher_own/pallas_call | solution.py:354
  18.8 0.1 collective-permute-start
  18.9 0.5 %collective-permute-start.3 = (bf16[2,128,256]{2,1,0:T(8,128)(2,1)S(1)}, bf16[2,128,256]{2,1,0:T(8,128)(2,1)S(1)}, u32[]{:S(2)}, u32[]{:S(2)}) collective-permute-start(bf16[2,128,256]{2,1,0:T(8,128)(2,1)S(1)} %get-tuple-element.39), channel_id=1, source_target_pairs={{0,1},{1,0},{2,3},{3,2},{4,5},{5,4},{6,7},{7,6},{8,9},{9,8},{10,11... | collective-permute-start | bytes 393224 | tf_op jit(solution)/shard_map/ppermute | solution.py:710
  19.4 3.3 %collective-permute-start.2 = (bf16[2,128,256]{2,1,0:T(8,128)(2,1)S(1)}, bf16[2,128,256]{2,1,0:T(8,128)(2,1)S(1)}, u32[]{:S(2)}, u32[]{:S(2)}) collective-permute-start(bf16[2,128,256]{2,1,0:T(8,128)(2,1)S(1)} %get-tuple-element.38), channel_id=1, source_target_pairs={{1,2},{3,4},{5,6},{7,8},{9,10},{11,12},{13,14},{2,1},{4,3},{6,5},{... | collective-permute-start | bytes 393224 | tf_op jit(solution)/shard_map/ppermute | solution.py:716
  22.7 0.0 copy-done
  22.7 0.0 copy-done.1
  22.7 2.4 %forward.1 = (f32[4,64,256]{2,1,0:T(8,128)S(1)}, f32[6,128,256]{2,1,0:T(8,128)S(1)}, bf16[3,6,128,256]{3,2,1,0:T(8,128)(2,1)S(1)}, bf16[256,1536]{1,0:T(8,128)(2...) custom-call(bf16[8,128,256]{2,1,0:T(8,128)(2,1)S(1)} %get-tuple-element.33.main_, ...), custom_call_target="tpu_custom_call" | custom-call | flops 4000000000 | bytes 3000000 | tf_op jit(solution)/shard_map/forward/pallas_call | solution.py:467
  25.1 0.0 collective-permute-done.3.pair_in
  25.1 1.7 %collective-permute-done.2.cross_in = bf16[2,128,256]{2,1,0:T(8,128)(2,1)S(1)} collective-permute-done((bf16[2,128,256]{2,1,0:T(8,128)(2,1)S(1)}, bf16[2,128,256]{2,1,0:T(8,128)(2,1)S(1)}, u32[]{:S(2)}, u32[]{:S(2)}) %collective-permute-start.2) | collective-permute-done | bytes 131104 | tf_op jit(solution)/shard_map/ppermute | solution.py:716
  26.8 0.0 collective-permute-done.1.from_cross_ref
  26.8 0.0 collective-permute-done.from_pair_ref
  26.8 1.4 %edge_grads.1 = (bf16[2,64,256]{2,1,0:T(8,128)(2,1)S(1)}, bf16[2,64,256]{2,1,0:T(8,128)(2,1)S(1)}, bf16[4,64,256]{2,1,0:T(8,128)(2,1)S(1)}, f32[4,128,256]{2,1,0:T(8,128)S(1)}) custom-call(bf16[8,128,256]{2,1,0:T(8,128)(2,1)S(1)} %get-tuple-element.33.main_ref, bf16[2,128,256]{2,1,0:T(8,128)(2,1)S(1)} %collective-permute-done.2.cross_in, ...), custom_call_target="tpu_custom_call" | custom-call | flops 2000000000 | bytes 3000000 | tf_op jit(solution)/shard_map/edge_grads/pallas_call | solution.py:532
  28.2 4.4 %collective-permute-start.4 = (bf16[2,64,256]{2,1,0:T(8,128)(2,1)S(1)}, bf16[2,64,256]{2,1,0:T(8,128)(2,1)S(1)}, u32[]{:S(2)}, u32[]{:S(2)}) collective-permute-start(bf16[2,64,256]{2,1,0:T(8,128)(2,1)S(1)} %get-tuple-element.48), channel_id=1, source_target_pairs={{1,2},{3,4},{5,6},{7,8},{9,10},{11,12},{13,14},{2,1},{4,3},{6,5},{... | collective-permute-start | bytes 196616 | tf_op jit(solution)/shard_map/ppermute | solution.py:716
  32.6 0.1 collective-permute-start.5
  32.7 2.1 %inner.1 = (f32[512,256]{1,0:T(8,128)}, f32[1024,128]{1,0:T(8,128)S(1)}, f32[1024,128]{1,0:T(8,128)S(1)}, bf16[3,6,128,256]{3,2,1,0:T(8,128)(2,1)S(1)}) custom-call(f32[8,64,256]{2,1,0:T(8,128)S(1)} %get-tuple-element.34.own_ref, f32[8,64,256]{2,1,0:T(8,128)S(1)} %collective-permute-done.from_pair_ref, ...), custom_call_target="tpu_custom_call" | custom-call | flops 4000000000 | bytes 3000000 | tf_op jit(solution)/shard_map/inner/pallas_call | solution.py:609
  34.7 0.0 collective-permute-done.4.cross_ref
  34.8 0.0 collective-permute-done.5.pair_ref
  34.8 2.4 %outer_rows.1 = f32[32,32,256]{2,1,0:T(8,128)} custom-call(bf16[4,64,256]{2,1,0:T(8,128)(2,1)S(1)} %get-tuple-element.43.grad_ref.main_ref, bf16[2,64,256]{2,1,0:T(8,128)(2,1)S(1)} %collective-permute-done.4.cross_ref, bf16[2,64,256]{2,1,0:T(8,128)(2,1)S(1)} %collective-permute-done.5.pair_ref, f32[4,128,256]{2,1,0:T(8,128)S(1)} %get-tuple-element.50.slope_ref, ...), custom_call_target="tpu_custom_call" | custom-call | flops 2000000000 | bytes 3000000 | tf_op jit(solution)/shard_map/outer_rows/pallas_call | solution.py:689
Async XLA Ops:
  7.7 19.1 %collective-permute-start.1 = (f32[8,64,256]{2,1,0:T(8,128)S(1)}, f32[8,64,256]{2,1,0:T(8,128)S(1)}, u32[]{:S(2)}, u32[]{:S(2)}) collective-permute-start(f32[8,64,256]{2,1,0:T(8,128)S(1)} %get-tuple-element.36), channel_id=1, source_target_pairs={{1,2},{3,4},{5,6},{7,8},{9,10},{11,12},{13,14},{2,1},{4,3},{6,5},{... | collective-permute-start | bytes 1572872 | tf_op jit(solution)/shard_map/ppermute | solution.py:716
  13.5 9.1 %copy-start = (bf16[32,32,3,3,3]{1,0,4,3,2:T(8,128)(2,1)S(1)}, bf16[32,32,3,3,3]{1,0,4,3,2:T(8,128)(2,1)}, u32[]{:S(2)}) copy-start(bf16[32,32,3,3,3]{1,0,4,3,2:T(8,128)(2,1)} %param.18) | copy-start | bytes 165892
  13.5 9.1 %copy-start.1 = (bf16[16,32,3,3,3]{1,0,4,3,2:T(8,128)(2,1)S(1)}, bf16[16,32,3,3,3]{1,0,4,3,2:T(8,128)(2,1)}, u32[]{:S(2)}) copy-start(bf16[16,32,3,3,3]{1,0,4,3,2:T(8,128)(2,1)} %param.19) | copy-start | bytes 82948
  18.8 8.0 %collective-permute-start = (f32[8,64,256]{2,1,0:T(8,128)S(1)}, f32[8,64,256]{2,1,0:T(8,128)S(1)}, u32[]{:S(2)}, u32[]{:S(2)}) collective-permute-start(f32[8,64,256]{2,1,0:T(8,128)S(1)} %get-tuple-element.35), channel_id=1, source_target_pairs={{0,1},{1,0},{2,3},{3,2},{4,5},{5,4},{6,7},{7,6},{8,9},{9,8},{10,11... | collective-permute-start | bytes 1572872 | tf_op jit(solution)/shard_map/ppermute | solution.py:710
  18.9 6.2 %collective-permute-start.3 = (bf16[2,128,256]{2,1,0:T(8,128)(2,1)S(1)}, bf16[2,128,256]{2,1,0:T(8,128)(2,1)S(1)}, u32[]{:S(2)}, u32[]{:S(2)}) collective-permute-start(bf16[2,128,256]{2,1,0:T(8,128)(2,1)S(1)} %get-tuple-element.39), channel_id=1, source_target_pairs={{0,1},{1,0},{2,3},{3,2},{4,5},{5,4},{6,7},{7,6},{8,9},{9,8},{10,11... | collective-permute-start | bytes 393224 | tf_op jit(solution)/shard_map/ppermute | solution.py:710
  19.4 7.4 %collective-permute-start.2 = (bf16[2,128,256]{2,1,0:T(8,128)(2,1)S(1)}, bf16[2,128,256]{2,1,0:T(8,128)(2,1)S(1)}, u32[]{:S(2)}, u32[]{:S(2)}) collective-permute-start(bf16[2,128,256]{2,1,0:T(8,128)(2,1)S(1)} %get-tuple-element.38), channel_id=1, source_target_pairs={{1,2},{3,4},{5,6},{7,8},{9,10},{11,12},{13,14},{2,1},{4,3},{6,5},{... | collective-permute-start | bytes 393224 | tf_op jit(solution)/shard_map/ppermute | solution.py:716
  28.2 6.5 %collective-permute-start.4 = (bf16[2,64,256]{2,1,0:T(8,128)(2,1)S(1)}, bf16[2,64,256]{2,1,0:T(8,128)(2,1)S(1)}, u32[]{:S(2)}, u32[]{:S(2)}) collective-permute-start(bf16[2,64,256]{2,1,0:T(8,128)(2,1)S(1)} %get-tuple-element.48), channel_id=1, source_target_pairs={{1,2},{3,4},{5,6},{7,8},{9,10},{11,12},{13,14},{2,1},{4,3},{6,5},{... | collective-permute-start | bytes 196616 | tf_op jit(solution)/shard_map/ppermute | solution.py:716
  32.6 2.2 %collective-permute-start.5 = (bf16[2,64,256]{2,1,0:T(8,128)(2,1)S(1)}, bf16[2,64,256]{2,1,0:T(8,128)(2,1)S(1)}, u32[]{:S(2)}, u32[]{:S(2)}) collective-permute-start(bf16[2,64,256]{2,1,0:T(8,128)(2,1)S(1)} %get-tuple-element.49), channel_id=1, source_target_pairs={{0,1},{1,0},{2,3},{3,2},{4,5},{5,4},{6,7},{7,6},{8,9},{9,8},{10,11... | collective-permute-start | bytes 196616 | tf_op jit(solution)/shard_map/ppermute | solution.py:710

commit v4 on v3

--- a/solution.py
+++ b/solution.py
@@ -147,13 +147,13 @@
     def before(op):
         kind, duo, q = op
         if kind == "hidden":
-            for r in range(q, q + 4):
+            for r in range(q, q + 3):
                 x_row(duo, r)
 
     def product(op):
         kind, duo, q = op
         if kind == "hidden":
-            big, data = big1, window(xbuf.at[duo], q, 4)
+            big, data = big1, window(xbuf.at[duo], q, 3)
         else:
             big, data = big2, window(hbuf.at[duo], q, 4)
         value[op] = jnp.dot(big[...], data, preferred_element_type=F32)
@@ -163,14 +163,13 @@
         out = value.pop(op)
         if kind == "hidden":
             hid = out * sigmoid(out)
-            for r in range(2):
-                for k in range(2):
-                    v = hid[r * 128 : (r + 1) * 128, k * lanes : (k + 1) * lanes]
-                    if q + r == 0:
-                        v = v * low_end[2 * duo + k]
-                    if q + r == 9:
-                        v = v * high_end[2 * duo + k]
-                    put_row(hbuf.at[duo], q + r, v, k * lanes)
+            for k in range(2):
+                v = hid[:, k * lanes : (k + 1) * lanes]
+                if q == 0:
+                    v = v * low_end[2 * duo + k]
+                if q == 9:
+                    v = v * high_end[2 * duo + k]
+                put_row(hbuf.at[duo], q, v, k * lanes)
             return
         for k in range(2):
             s = 2 * duo + k
@@ -193,7 +192,7 @@
     order = []
     late = []
     for duo in range(slots // 2):
-        for q in range(0, 10, 2):
+        for q in range(10):
             order.append(("hidden", duo, q))
             if late:
                 order.append(late.pop(0))
@@ -247,7 +246,9 @@
     total[...] = jnp.zeros_like(total)
     for copy in copies:
         copy.wait()
-    fill_big(big1, band(w1_ref, False), 2)
+    for load in loads[:2]:
+        load.wait()
+    fill_big(big1, band(w1_ref, False), 1)
     fill_big(big2, band(w2_ref, True), 2)
 
     def store(mine, row, low, high):
@@ -258,7 +259,7 @@
     teacher_half(
         False,
         (brick_s, z_s, count_s),
-        lambda s: loads[s].wait(),
+        lambda s: loads[s].wait() if s >= 2 else None,
         feats_ref,
         gauss_ref,
         big1,
@@ -340,7 +341,7 @@
         out_shape=[
             SUMS,
             jax.ShapeDtypeStruct((2, 8, 64, 256), F32),
-            jax.ShapeDtypeStruct((256, 1536), BF16),
+            jax.ShapeDtypeStruct((128, 1152), BF16),
             jax.ShapeDtypeStruct((128, 1536), BF16),
             jax.ShapeDtypeStruct(feats.shape, BF16),
             jax.ShapeDtypeStruct(gauss.shape, F32),
@@ -436,8 +437,14 @@
     return pre * sig, sig * (1.0 + pre * (1.0 - sig))
 
 
+def two_rows(big_ref, first):
+    return jnp.concatenate(
+        [big_ref[:, pl.ds((4 * d + first) * 128, 256)] for d in range(3)], axis=1
+    )
+
+
 def forward_kernel(
-    main_ref, w1_ref, w2_ref, prob_ref, slope_ref, hbuf, big1, big2, back1, back2, xbuf
+    main_ref, w1_ref, w2_ref, prob_ref, slope_ref, hbuf, part_ref, big1, big2, back1, back2, xbuf
 ):
     fill_big(big1, band(w1_ref, False), 2)
     fill_big(big2, band(w2_ref, True), 2)
@@ -457,6 +464,10 @@
         logits = jnp.dot(big2[...], window(hbuf, y, 4), preferred_element_type=F32)
         for k in range(2):
             prob_ref[y + k] = class_softmax(logits[k * 64 : (k + 1) * 64])
+    for i, (first, y) in enumerate(((2, 0), (0, 6))):
+        part_ref[i] = jnp.dot(
+            two_rows(big1, first), window(xbuf, y, 2), preferred_element_type=F32
+        )
     flip2 = band(w2_ref, True)
     fill_big(back2, [flip2[8 - t].T for t in range(9)], 2)
     flip1 = band(w1_ref, True)
@@ -468,11 +479,12 @@
         forward_kernel,
         name="forward",
         in_specs=[VMEM] * 3,
-        out_specs=[VMEM] * 7,
+        out_specs=[VMEM] * 8,
         out_shape=[
             jax.ShapeDtypeStruct((4, 64, 256), F32),
             jax.ShapeDtypeStruct((6, 128, 256), F32),
             jax.ShapeDtypeStruct((3, 6, 128, 256), BF16),
+            jax.ShapeDtypeStruct((2, 256, 256), F32),
             jax.ShapeDtypeStruct((256, 1536), BF16),
             jax.ShapeDtypeStruct((128, 1536), BF16),
             jax.ShapeDtypeStruct((256, 1536), BF16),
@@ -485,7 +497,7 @@
 
 
 def edge_kernel(
-    main_ref,
+    part_ref,
     cross_in,
     pair_in,
     hin_ref,
@@ -501,14 +513,15 @@
     xbuf,
     hbuf,
 ):
-    put_edges(lambda y, v: put_row(xbuf, y, v), pair_in, cross_in, 0, 6)
-    for y, row in ((2, 0), (3, 1), (4, 6), (5, 7)):
-        put_row(xbuf, y, main_ref[row].astype(F32))
+    put_edges(lambda y, v: put_row(xbuf, y, v), pair_in, cross_in, 0, 2)
     for d in range(3):
         hbuf[d, pl.ds(2, 2)] = hin_ref[d, pl.ds(0, 2)]
         hbuf[d, pl.ds(4, 2)] = hin_ref[d, pl.ds(4, 2)]
     for g, h, row in ((0, 0, -1), (4, 6, 7)):
-        pre = jnp.dot(big1[...], window(xbuf, g, 4), preferred_element_type=F32)
+        half = g // 2
+        pre = part_ref[half // 2] + jnp.dot(
+            two_rows(big1, half), window(xbuf, half, 2), preferred_element_type=F32
+        )
         hid, slope = activate(pre)
         for k in range(2):
             rows = slice(k * 128, (k + 1) * 128)
@@ -527,7 +540,7 @@
     cross_ref[...] = grad_ref[pl.ds(2 * odd, 2)]
 
 
-def edge_grads(main, cross, pair, hidden, big1, big2, own, from_pair, from_cross):
+def edge_grads(part, cross, pair, hidden, big1, big2, own, from_pair, from_cross):
     edge = jax.ShapeDtypeStruct((2, 64, 256), BF16)
     return pl.pallas_call(
         edge_kernel,
@@ -541,12 +554,12 @@
             jax.ShapeDtypeStruct((4, 128, 256), F32),
         ],
         scratch_shapes=[
-            pltpu.VMEM((3, 8, 128, 256), BF16),
+            pltpu.VMEM((3, 4, 128, 256), BF16),
             pltpu.VMEM((3, 8, 128, 256), BF16),
         ],
         compiler_params=params(12),
         cost_estimate=cost(2_000_000_000, 3_000_000),
-    )(main, cross, pair, hidden, big1, big2, own, from_pair, from_cross)
+    )(part, cross, pair, hidden, big1, big2, own, from_pair, from_cross)
 
 
 def put_out(turns, y, grad):
@@ -747,10 +760,10 @@
     )
     got_pair = swap_pair(sum_pair)
     edge_pair = swap_pair(to_pair)
-    prob, slope, hidden, near1, near2, back1, back2 = forward(main, sw1, sw2)
+    prob, slope, hidden, part, near1, near2, back1, back2 = forward(main, sw1, sw2)
     sums = (own, got_pair, got_cross)
     grad_pair, grad_cross, grad, slope_ends = edge_grads(
-        main, edge_cross, edge_pair, hidden, near1, near2, *sums
+        part, edge_cross, edge_pair, hidden, near1, near2, *sums
     )
     near_pair = swap_pair(grad_pair)
     near_cross = swap_cross(grad_cross)

time: 37.9 us -> 37.7 us (level)
  Pallas kernels: 21.8 us -> 21.4 us
where the time goes in v4:
time: 37.7 us; the launch traced here: 37 us
  Pallas kernels  21.4 us (57%)
  starting transfers between devices  12.9 us (34%)
  waiting for transfers between devices  1.81 us (5%)
  between operations  0.93 us (2%)
    ppermute x3, starting transfers between devices, swap_cross(): return lax.ppermute(value, 'gy', pairs + [(j, i) for i, j in pairs])  12.2 us
    pallas_call x1, Pallas kernels, teacher_outer(): pl.pallas_call(outer_kernel, name='teacher_outer', grid_spec=pltpu.Prefet...  7 us
    pallas_call x1, Pallas kernels, teacher_own(): pl.pallas_call(own_kernel, name='teacher_own', grid_spec=pltpu.PrefetchSc...  4.97 us
    pallas_call x1, Pallas kernels, forward(): pl.pallas_call(forward_kernel, name='forward', in_specs=[VMEM] * 3, out_s...  2.6 us
    pallas_call x1, Pallas kernels, outer_rows(): pl.pallas_call(outer_rows_kernel, name='outer_rows', in_specs=[VMEM] * 9,...  2.36 us
    pallas_call x1, Pallas kernels, inner(): pl.pallas_call(inner_kernel, name='inner', in_specs=[VMEM] * 8, out_specs...  2.06 us
    ppermute x3, waiting for transfers between devices, swap_cross(): return lax.ppermute(value, 'gy', pairs + [(j, i) for i, j in pairs])  1.8 us
    pallas_call x1, Pallas kernels, relay(): pl.pallas_call(relay_kernel, name='relay', in_specs=[HBM, VMEM], out_spec...  1.22 us
  transfers between devices with their start and end apart: 6, of which 1 were waited for; matrix products, arithmetic and copies ran while one was open for 0% of the time, Pallas kernels for 29%

profile of v4, /device:TPU:1, one launch (start us, length us, event | category | flops | bytes accessed | tf_op | source)
XLA Modules:
  0.0 37.0 jit_solution(4390075666326025813)
XLA Ops:
  0.6 7.0 %teacher_outer.1 = (f32[8,64,256]{2,1,0:T(8,128)S(1)}, f32[2,8,64,256]{3,2,1,0:T(8,128)S(1)}, bf16[128,1152]{1,0:T(8,128)(2,1)S(1)}, bf16[128,1536]{1,0:T(8,128)...) custom-call(s32[64]{0:T(128)} %brick_s.3, s32[64]{0:T(128)} %z_s.3, s32[16]{0:T(128)} %count_s.3, ...), custom_call_target="tpu_custom_call" | custom-call | flops 5000000000 | bytes 4000000 | tf_op jit(solution)/shard_map/teacher_outer/pallas_call | solution.py:330
  7.6 4.5 %collective-permute-start.1 = (f32[8,64,256]{2,1,0:T(8,128)S(1)}, f32[8,64,256]{2,1,0:T(8,128)S(1)}, u32[]{:S(2)}, u32[]{:S(2)}) collective-permute-start(f32[8,64,256]{2,1,0:T(8,128)S(1)} %get-tuple-element.37), channel_id=1, source_target_pairs={{1,2},{3,4},{5,6},{7,8},{9,10},{11,12},{13,14},{2,1},{4,3},{6,5},{... | collective-permute-start | bytes 1572872 | tf_op jit(solution)/shard_map/ppermute | solution.py:729
  12.2 1.2 %relay.1 = (bf16[8,128,256]{2,1,0:T(8,128)(2,1)S(1)}, bf16[2,128,256]{2,1,0:T(8,128)(2,1)S(1)}) custom-call(bf16[1024,256]{1,0:T(8,128)(2,1)} %bitcast.18, f32[4,16,128]{2,1,0:T(8,128)S(1)} %get-tuple-element.30.behind.gauss_ref), custom_call_target="tpu_custom_call" | custom-call | bytes 1500000 | tf_op jit(solution)/shard_map/relay/pallas_call | solution.py:391
  13.4 0.0 copy-start
  13.4 0.0 copy-start.1
  13.5 5.0 %teacher_own.1 = (f32[8,64,256]{2,1,0:T(8,128)S(1)}, f32[8,64,256]{2,1,0:T(8,128)S(1)}, bf16[2,128,256]{2,1,0:T(8,128)(2,1)S(1)}) custom-call(s32[64]{0:T(128)} %brick_s.3, s32[64]{0:T(128)} %z_s.3, s32[16]{0:T(128)} %count_s.3, bf16[4,2048,128]{2,1,0:T(8,128)(2,1)S(1)} %get-tuple-element.29.feats_ref, f32[4,16,128]{2,1,0:T(8,128)S(1)} %get-tuple-element.30.behind.gauss_ref, ...), custom_call_target="tpu_custom_call" | custom-call | flops 4000000000 | bytes 3000000 | tf_op jit(solution)/shard_map/teacher_own/pallas_call | solution.py:355
  18.4 0.1 collective-permute-start
  18.5 0.5 %collective-permute-start.3 = (bf16[2,128,256]{2,1,0:T(8,128)(2,1)S(1)}, bf16[2,128,256]{2,1,0:T(8,128)(2,1)S(1)}, u32[]{:S(2)}, u32[]{:S(2)}) collective-permute-start(bf16[2,128,256]{2,1,0:T(8,128)(2,1)S(1)} %get-tuple-element.41), channel_id=1, source_target_pairs={{0,1},{1,0},{2,3},{3,2},{4,5},{5,4},{6,7},{7,6},{8,9},{9,8},{10,11... | collective-permute-start | bytes 393224 | tf_op jit(solution)/shard_map/ppermute | solution.py:723
  19.0 3.3 %collective-permute-start.2 = (bf16[2,128,256]{2,1,0:T(8,128)(2,1)S(1)}, bf16[2,128,256]{2,1,0:T(8,128)(2,1)S(1)}, u32[]{:S(2)}, u32[]{:S(2)}) collective-permute-start(bf16[2,128,256]{2,1,0:T(8,128)(2,1)S(1)} %get-tuple-element.40), channel_id=1, source_target_pairs={{1,2},{3,4},{5,6},{7,8},{9,10},{11,12},{13,14},{2,1},{4,3},{6,5},{... | collective-permute-start | bytes 393224 | tf_op jit(solution)/shard_map/ppermute | solution.py:729
  22.3 0.0 copy-done
  22.3 0.0 copy-done.1
  22.3 2.6 %forward.1 = (f32[4,64,256]{2,1,0:T(8,128)S(1)}, f32[6,128,256]{2,1,0:T(8,128)S(1)}, bf16[3,6,128,256]{3,2,1,0:T(8,128)(2,1)S(1)}, f32[2,256,256]{2,1,0:T(8,128)...) custom-call(bf16[8,128,256]{2,1,0:T(8,128)(2,1)S(1)} %get-tuple-elem, ...), custom_call_target="tpu_custom_call" | custom-call | flops 4000000000 | bytes 3000000 | tf_op jit(solution)/shard_map/forward/pallas_call | solution.py:478
  24.9 0.0 collective-permute-done.3.pair_in
  24.9 1.8 %collective-permute-done.2.cross_in = bf16[2,128,256]{2,1,0:T(8,128)(2,1)S(1)} collective-permute-done((bf16[2,128,256]{2,1,0:T(8,128)(2,1)S(1)}, bf16[2,128,256]{2,1,0:T(8,128)(2,1)S(1)}, u32[]{:S(2)}, u32[]{:S(2)}) %collective-permute-start.2) | collective-permute-done | bytes 131104 | tf_op jit(solution)/shard_map/ppermute | solution.py:729
  26.7 0.0 collective-permute-done.1.from_cross_ref
  26.7 0.0 collective-permute-done.from_pair_ref
  26.7 1.2 %edge_grads.1 = (bf16[2,64,256]{2,1,0:T(8,128)(2,1)S(1)}, bf16[2,64,256]{2,1,0:T(8,128)(2,1)S(1)}, bf16[4,64,256]{2,1,0:T(8,128)(2,1)S(1)}, f32[4,128,256]{2,1,0:T(8,128)S(1)}) custom-call(f32[2,256,256]{2,1,0:T(8,128)S(1)} %get-tuple-element.39.part_ref, bf16[2,128,256]{2,1,0:T(8,128)(2,1)S(1)} %collective-permute-done.2.cross_in, ...), custom_call_target="tpu_custom_call" | custom-call | flops 2000000000 | bytes 3000000 | tf_op jit(solution)/shard_map/edge_grads/pallas_call | solution.py:545
  27.9 4.4 %collective-permute-start.4 = (bf16[2,64,256]{2,1,0:T(8,128)(2,1)S(1)}, bf16[2,64,256]{2,1,0:T(8,128)(2,1)S(1)}, u32[]{:S(2)}, u32[]{:S(2)}) collective-permute-start(bf16[2,64,256]{2,1,0:T(8,128)(2,1)S(1)} %get-tuple-element.50), channel_id=1, source_target_pairs={{1,2},{3,4},{5,6},{7,8},{9,10},{11,12},{13,14},{2,1},{4,3},{6,5},{... | collective-permute-start | bytes 196616 | tf_op jit(solution)/shard_map/ppermute | solution.py:729
  32.3 0.1 collective-permute-start.5
  32.4 2.1 %inner.1 = (f32[512,256]{1,0:T(8,128)}, f32[1024,128]{1,0:T(8,128)S(1)}, f32[1024,128]{1,0:T(8,128)S(1)}, bf16[3,6,128,256]{3,2,1,0:T(8,128)(2,1)S(1)}) custom-call(f32[8,64,256]{2,1,0:T(8,128)S(1)} %get-tuple-element.35.own_ref, f32[8,64,256]{2,1,0:T(8,128)S(1)} %collective-permute-done.from_pair_ref, ...), custom_call_target="tpu_custom_call" | custom-call | flops 4000000000 | bytes 3000000 | tf_op jit(solution)/shard_map/inner/pallas_call | solution.py:622
  34.5 0.0 collective-permute-done.4.cross_ref
  34.5 0.0 collective-permute-done.5.pair_ref
  34.5 2.4 %outer_rows.1 = f32[32,32,256]{2,1,0:T(8,128)} custom-call(bf16[4,64,256]{2,1,0:T(8,128)(2,1)S(1)} %get-tuple-element.45.grad_ref.main_ref, bf16[2,64,256]{2,1,0:T(8,128)(2,1)S(1)} %collective-permute-done.4.cross_ref, bf16[2,64,256]{2,1,0:T(8,128)(2,1)S(1)} %collective-permute-done.5.pair_ref, f32[4,128,256]{2,1,0:T(8,128)S(1)} %get-tuple-element.52.slope_ref, ...), custom_call_target="tpu_custom_call" | custom-call | flops 2000000000 | bytes 3000000 | tf_op jit(solution)/shard_map/outer_rows/pallas_call | solution.py:702
Async XLA Ops:
  7.6 19.1 %collective-permute-start.1 = (f32[8,64,256]{2,1,0:T(8,128)S(1)}, f32[8,64,256]{2,1,0:T(8,128)S(1)}, u32[]{:S(2)}, u32[]{:S(2)}) collective-permute-start(f32[8,64,256]{2,1,0:T(8,128)S(1)} %get-tuple-element.37), channel_id=1, source_target_pairs={{1,2},{3,4},{5,6},{7,8},{9,10},{11,12},{13,14},{2,1},{4,3},{6,5},{... | collective-permute-start | bytes 1572872 | tf_op jit(solution)/shard_map/ppermute | solution.py:729
  13.4 8.9 %copy-start = (bf16[32,32,3,3,3]{1,0,4,3,2:T(8,128)(2,1)S(1)}, bf16[32,32,3,3,3]{1,0,4,3,2:T(8,128)(2,1)}, u32[]{:S(2)}) copy-start(bf16[32,32,3,3,3]{1,0,4,3,2:T(8,128)(2,1)} %param.18) | copy-start | bytes 165892
  13.4 8.9 %copy-start.1 = (bf16[16,32,3,3,3]{1,0,4,3,2:T(8,128)(2,1)S(1)}, bf16[16,32,3,3,3]{1,0,4,3,2:T(8,128)(2,1)}, u32[]{:S(2)}) copy-start(bf16[16,32,3,3,3]{1,0,4,3,2:T(8,128)(2,1)} %param.19) | copy-start | bytes 82948
  18.4 8.3 %collective-permute-start = (f32[8,64,256]{2,1,0:T(8,128)S(1)}, f32[8,64,256]{2,1,0:T(8,128)S(1)}, u32[]{:S(2)}, u32[]{:S(2)}) collective-permute-start(f32[8,64,256]{2,1,0:T(8,128)S(1)} %get-tuple-element.36), channel_id=1, source_target_pairs={{0,1},{1,0},{2,3},{3,2},{4,5},{5,4},{6,7},{7,6},{8,9},{9,8},{10,11... | collective-permute-start | bytes 1572872 | tf_op jit(solution)/shard_map/ppermute | solution.py:723
  18.5 6.4 %collective-permute-start.3 = (bf16[2,128,256]{2,1,0:T(8,128)(2,1)S(1)}, bf16[2,128,256]{2,1,0:T(8,128)(2,1)S(1)}, u32[]{:S(2)}, u32[]{:S(2)}) collective-permute-start(bf16[2,128,256]{2,1,0:T(8,128)(2,1)S(1)} %get-tuple-element.41), channel_id=1, source_target_pairs={{0,1},{1,0},{2,3},{3,2},{4,5},{5,4},{6,7},{7,6},{8,9},{9,8},{10,11... | collective-permute-start | bytes 393224 | tf_op jit(solution)/shard_map/ppermute | solution.py:723
  19.0 7.7 %collective-permute-start.2 = (bf16[2,128,256]{2,1,0:T(8,128)(2,1)S(1)}, bf16[2,128,256]{2,1,0:T(8,128)(2,1)S(1)}, u32[]{:S(2)}, u32[]{:S(2)}) collective-permute-start(bf16[2,128,256]{2,1,0:T(8,128)(2,1)S(1)} %get-tuple-element.40), channel_id=1, source_target_pairs={{1,2},{3,4},{5,6},{7,8},{9,10},{11,12},{13,14},{2,1},{4,3},{6,5},{... | collective-permute-start | bytes 393224 | tf_op jit(solution)/shard_map/ppermute | solution.py:729
  27.9 6.5 %collective-permute-start.4 = (bf16[2,64,256]{2,1,0:T(8,128)(2,1)S(1)}, bf16[2,64,256]{2,1,0:T(8,128)(2,1)S(1)}, u32[]{:S(2)}, u32[]{:S(2)}) collective-permute-start(bf16[2,64,256]{2,1,0:T(8,128)(2,1)S(1)} %get-tuple-element.50), channel_id=1, source_target_pairs={{1,2},{3,4},{5,6},{7,8},{9,10},{11,12},{13,14},{2,1},{4,3},{6,5},{... | collective-permute-start | bytes 196616 | tf_op jit(solution)/shard_map/ppermute | solution.py:729
  32.3 2.2 %collective-permute-start.5 = (bf16[2,64,256]{2,1,0:T(8,128)(2,1)S(1)}, bf16[2,64,256]{2,1,0:T(8,128)(2,1)S(1)}, u32[]{:S(2)}, u32[]{:S(2)}) collective-permute-start(bf16[2,64,256]{2,1,0:T(8,128)(2,1)S(1)} %get-tuple-element.51), channel_id=1, source_target_pairs={{0,1},{1,0},{2,3},{3,2},{4,5},{5,4},{6,7},{7,6},{8,9},{9,8},{10,11... | collective-permute-start | bytes 196616 | tf_op jit(solution)/shard_map/ppermute | solution.py:723
